TPU v7x, 256 devices: a whole 4x4x8 slice. The times are simulated.
256 devices in a mesh: seq: 32 (over z, y), head: 8 (over x, core).
Axes of the slice: x: 4, y: 4, z: 8, core: 2. Of those that a mesh axis runs over, the one named last changes fastest.
Arguments:
- hidden_states: bfloat16 [8, 5, 8192], P(None, None, 'seq'), may hold values from -6 to 6
- w_query: bfloat16 [8192, 8192], P('seq', 'head'), may hold values from -0.0625 to 0.0625
- w_key: bfloat16 [8192, 1024], P('seq', 'head'), may hold values from -0.15625 to 0.15625
- w_value: bfloat16 [8192, 1024], P('seq', 'head'), may hold values from -0.0625 to 0.0625
- w_out: bfloat16 [8192, 8192], P('head', 'seq'), may hold values from -0.0625 to 0.0625
- key_cache: bfloat16 [8, 32768, 1024], P(None, 'seq', 'head'), may hold values from -104 to 104
- value_cache: bfloat16 [8, 32768, 1024], P(None, 'seq', 'head'), may hold values from -6 to 6
- context_lengths: int32 [8], replicated, may hold values from 8192 to 32768, as said below
- keep_blocks: int32 [8, 256], P(None, 'seq'), may hold values from 0 to 1, as said below
Outputs:
- verify_out: bfloat16 [8, 5, 8192], P(None, None, 'seq')
- draft_out: bfloat16 [8, 4, 8192], P(None, None, 'seq')
Inputs may be any that keep to these rules, and one draw needn't show every extreme that they name: `keep_blocks`: block 0 of every sequence is kept. `context_lengths`: one sequence has length 32768.
All inputs are finite; a program needn't handle non-finite values.
Results may differ from a plain program's by a relative error of at most 0.017.
Values may be sent and summed in bfloat16 or wider, within the bound.
No kernel may reach another device: no remote copies, remote signals or barrier semaphores. Data moves between devices by JAX's collectives and lax.ppermute only.
A program may use at most 64 MiB of HBM per device.

v0:
```python
import jax
import jax.numpy as jnp
from jax import lax
from jax.sharding import PartitionSpec as P

HEAD_DIM = 128
BLOCK = 128


big_negative = -1e30


def rotate(values_in, positions):
    half_dim = HEAD_DIM // 2
    inverse = 500000.0 ** (-(jnp.arange(half_dim, dtype=jnp.float32) * 2.0) / HEAD_DIM)
    angles = positions[:, :, None, None].astype(jnp.float32) * inverse
    cosine = jnp.cos(angles)
    sine = jnp.sin(angles)
    first_half = values_in[..., :half_dim]
    second_half = values_in[..., half_dim:]
    return jnp.concatenate(
        [first_half * cosine - second_half * sine, second_half * cosine + first_half * sine],
        axis=-1,
    )


def partial_softmax(scores, mask_full, cache_values):
    masked = jnp.where(mask_full, scores, big_negative)
    peak_value = jnp.max(masked, axis=-1)
    weights = jnp.where(mask_full, jnp.exp(masked - peak_value[..., None]), 0.0)
    weighted = jnp.einsum(
        "bkjgt,btkd->bkjgd",
        weights.astype(jnp.bfloat16),
        cache_values,
        preferred_element_type=jnp.float32,
    )
    return (peak_value, jnp.sum(weights, axis=-1), weighted)


def finish(partials, new_scores, causal, new_values):
    peak_cache, total_sum, weighted = partials
    mask_full = causal[None, None, :, None, :]
    masked = jnp.where(mask_full, new_scores, big_negative)
    peak_value = jnp.maximum(peak_cache, jnp.max(masked, axis=-1))
    factor_old = jnp.exp(peak_cache - peak_value)
    weights = jnp.where(mask_full, jnp.exp(masked - peak_value[..., None]), 0.0)
    total_sum = total_sum * factor_old + jnp.sum(weights, axis=-1)
    weighted = weighted * factor_old[..., None] + jnp.einsum(
        "bkjgi,bikd->bkjgd",
        weights.astype(jnp.bfloat16),
        new_values,
        preferred_element_type=jnp.float32,
    )
    result = weighted / total_sum[..., None]
    batch_size, kv_local, positions_count, group_size, head_size = result.shape
    return result.transpose(0, 2, 1, 3, 4).reshape(
        batch_size * positions_count, kv_local * group_size * head_size
    )


def per_device(
    hidden_states,
    w_query,
    w_key,
    w_value,
    w_out,
    key_cache,
    value_cache,
    context_lengths,
    keep_blocks,
):
    seq_index = lax.axis_index("seq")
    batch_size, verify, width_local = hidden_states.shape
    draft_len = verify - 1
    kv_local = key_cache.shape[2] // HEAD_DIM
    heads_local = w_query.shape[1] // HEAD_DIM
    group_size = heads_local // kv_local
    ctx_local = key_cache.shape[1]
    score_scale = HEAD_DIM ** (-0.5)
    tok_rows = hidden_states.reshape(batch_size * verify, width_local)
    query_part = jnp.dot(tok_rows, w_query, preferred_element_type=jnp.float32)
    key_part = jnp.dot(tok_rows, w_key, preferred_element_type=jnp.float32)
    value_part = jnp.dot(tok_rows, w_value, preferred_element_type=jnp.float32)
    query_sum, key_sum, value_sum = lax.psum((query_part, key_part, value_part), "seq")
    positions = context_lengths[:, None] + jnp.arange(verify, dtype=jnp.int32)[None, :]
    query_rot = rotate(
        query_sum.reshape(batch_size, verify, heads_local, HEAD_DIM), positions
    ).astype(jnp.bfloat16)
    new_key = rotate(key_sum.reshape(batch_size, verify, kv_local, HEAD_DIM), positions).astype(
        jnp.bfloat16
    )
    new_values = value_sum.reshape(batch_size, verify, kv_local, HEAD_DIM).astype(jnp.bfloat16)
    grouped = query_rot.reshape(batch_size, verify, kv_local, group_size, HEAD_DIM)
    cache_keys = key_cache.reshape(batch_size, ctx_local, kv_local, HEAD_DIM)
    cache_values = value_cache.reshape(batch_size, ctx_local, kv_local, HEAD_DIM)
    scores = (
        jnp.einsum("bjkgd,btkd->bkjgt", grouped, cache_keys, preferred_element_type=jnp.float32)
        * score_scale
    )
    key_positions = seq_index * ctx_local + jnp.arange(ctx_local, dtype=jnp.int32)
    live_mask = key_positions[None, :] < context_lengths[:, None]
    kept_mask = live_mask & (jnp.repeat(keep_blocks, BLOCK, axis=1) > 0)
    target_peak, target_total, target_weighted = partial_softmax(
        scores, live_mask[:, None, None, None, :], cache_values
    )
    draft_peak, draft_total, draft_weighted = partial_softmax(
        scores[:, :, :draft_len], kept_mask[:, None, None, None, :], cache_values
    )
    peak_target, peak_draft = lax.pmax((target_peak, draft_peak), "seq")
    factor_target = jnp.exp(target_peak - peak_target)
    factor_draft = jnp.exp(draft_peak - peak_draft)
    sum_parts = lax.psum(
        (
            target_total * factor_target,
            target_weighted * factor_target[..., None],
            draft_total * factor_draft,
            draft_weighted * factor_draft[..., None],
        ),
        "seq",
    )
    merged = (peak_target, sum_parts[0], sum_parts[1], peak_draft, sum_parts[2], sum_parts[3])
    causal = jnp.arange(verify)[None, :] <= jnp.arange(verify)[:, None]
    new_scores = (
        jnp.einsum("bjkgd,bikd->bkjgi", grouped, new_key, preferred_element_type=jnp.float32)
        * score_scale
    )
    target_heads = finish(merged[0:3], new_scores, causal, new_values)
    draft_heads = finish(merged[3:6], new_scores[:, :, :draft_len], causal[:draft_len], new_values)
    attended = jnp.concatenate([target_heads, draft_heads], axis=0).astype(jnp.bfloat16)
    projected = jnp.dot(attended, w_out, preferred_element_type=jnp.float32)
    summed = lax.psum(projected.astype(jnp.bfloat16), "head")
    verify_out = summed[: batch_size * verify].reshape(batch_size, verify, summed.shape[1])
    draft_out = summed[batch_size * verify :].reshape(batch_size, draft_len, summed.shape[1])
    return (verify_out, draft_out)


def solution(mesh):
    placed = (
        P(None, None, "seq"),
        P("seq", "head"),
        P("seq", "head"),
        P("seq", "head"),
        P("head", "seq"),
        P(None, "seq", "head"),
        P(None, "seq", "head"),
        P(),
        P(None, "seq"),
    )
    return jax.shard_map(
        per_device,
        mesh=mesh,
        in_specs=placed,
        out_specs=(P(None, None, "seq"), P(None, None, "seq")),
        check_vma=False,
    )
```

profile of v0, /device:TPU:1, one launch (start us, length us, event | category | flops | bytes accessed | tf_op | source)
XLA Modules:
  0.0 633.8 jit_solution(9448252033808468446)
XLA Ops:
  7.2 0.0 copy-start
  7.2 0.0 all-reduce.6.cloned.1.call-start
  7.3 0.9 copy.42
  8.2 1.2 convolution_bitcast_fusion
  9.4 0.7 copy.58
  10.1 0.0 all-reduce.6.cloned.1.call-update
  10.1 0.0 all-reduce.8.cloned.1.call-start
  10.2 0.0 copy-done.19
  10.2 0.0 copy-start.16
  10.3 0.1 add_convert_fusion.1
  10.3 0.1 copy.48
  10.4 0.1 fusion.87
  10.6 0.6 reshape.256
  11.2 0.0 copy-done.12
  11.2 0.7 fusion.88
  11.9 0.0 copy-done.16
  11.9 0.6 slice.34
  12.5 0.2 multiply_cosine_fusion.1
  12.7 0.1 broadcast_compare_fusion
  12.8 0.0 copy-start.10
  12.8 0.0 copy-start.8
  12.8 141.8 %all-reduce.6.cloned.1.call-done = f32[8,5,8,128]{3,2,1,0:T(8,128)} async-done(((f32[8,5,8,128]{3,2,1,0:T(8,128)}), f32[8,5,8,128]{3,2,1,0:T(8,128)}) %all-reduce.6.cloned.1.call-update) | async-done | bytes 163856 | tf_op jit(solution)/shard_map/psum | solution.py:84
  154.6 1.1 subtract_convert_fusion
  155.7 0.0 copy-start.1
  155.8 0.0 copy-done.18
  155.8 0.0 copy-done.13
  155.8 0.0 copy-done
  155.8 0.9 select_reduce_fusion
  156.7 1.0 fusion.27
  157.8 0.2 fusion.29
  158.0 0.0 copy-start.5
  158.0 1.0 fusion.30
  159.0 0.0 copy-done.5
  159.0 112.7 %all-reduce.2 = (f32[8,1,4,8]{3,2,0,1:T(4,128)}, f32[8,1,5,8]{3,2,0,1:T(8,128)S(1)}) all-reduce(f32[8,1,4,8]{3,2,0,1:T(4,128)} %bitcast.153, f32[8,1,5,8]{3,2,0,1:T(8,128)S(1)} %bitcast.151), channel_id=1, replica_groups=mesh['seq'=32,'head'=8] {'seq'}, use_global_device_ids=true, to_apply=%region_11.12 | all-reduce | flops 576 | bytes 4608 | tf_op jit(solution)/shard_map/pmax | solution.py:109
  271.7 1.4 bitcast_multiply_fusion
  273.1 1.4 bitcast_multiply_fusion.1
  274.5 111.8 %all-reduce = (f32[8,5,1,128]{3,1,0,2:T(8,128)}, f32[8,1,4,8]{3,2,0,1:T(4,128)}, bf16[40,128]{1,0:T(8,128)(2,1)}, f32[8,1,5,8]{3,2,0,1:T(8,128)}) all-reduce(f32[8,5,1,128]{3,1,0,2:T(8,128)} %reshape.256, f32[8,1,4,8]{3,2,0,1:T(4,128)} %get-tuple-element.35, f32[40,128]{1,0:T(8,128)} %fusion.88, ...), channel_id=1, replica_groups=mesh['seq'=32,'head'=8] {'seq'}, use_global_device_ids=true, to_apply=%region_4.5 | all-reduce | flops 10816 | bytes 76288 | tf_op jit(solution)/shard_map/psum | solution.py:84
  386.3 1.0 fusion.73
  387.3 1.4 fusion.66
  388.7 0.8 select_reduce_fusion.1
  389.4 0.0 copy-start.7
  389.5 0.0 copy-done.3
  389.5 0.6 copy-done.7
  390.1 2.0 fusion.47
  392.1 3.0 fusion.12
  395.0 0.0 copy-done.20
  395.1 0.0 copy-start.15
  395.1 0.0 copy-start.4
  395.1 1.2 fusion.20
  396.3 0.8 fusion.49
  397.1 0.7 fusion.75
  397.8 0.8 fusion.51
  398.6 0.0 all-reduce.8.cloned.1.call-update
  398.6 0.0 copy-start.2
  398.7 0.8 fusion.78
  399.5 0.8 fusion.74
  400.3 196.9 %all-reduce.8.cloned.1.call-done = (f32[8,1,4,8,128]{4,3,2,0,1:T(8,128)}, f32[8,1,5,8,128]{4,3,2,0,1:T(8,128)}) async-done(((f32[8,1,4,8,128]{4,3,2,0,1:T(8,128)}, f32[8,1,5,8,128]{4,3,2,0,1:T(8,128)}), (f32[8,1,4,8,128]{4,3,2,0,1:T(8,128)}, f32[8,1,5,8,128]{4,3,2,0,1:T(8,128)})) %all-reduce.8.cloned.1.call-update) | async-done | bytes 294928 | tf_op jit(solution)/shard_map/psum | solution.py:112
  597.2 1.2 fusion.23
  598.4 1.1 fusion.26
  599.6 0.0 copy-done.2
  599.6 0.2 convolution_convert_fusion
  599.8 25.9 %psum.63 = bf16[72,256]{1,0:T(8,128)(2,1)S(1)} all-reduce(bf16[72,256]{1,0:T(8,128)(2,1)S(1)} %convolution_convert_fusion), channel_id=1, replica_groups=mesh['seq'=32,'head'=8] {'head'}, use_global_device_ids=true, to_apply=%region_17.18 | all-reduce | flops 18432 | bytes 73728 | tf_op jit(solution)/shard_map/psum | solution.py:131
  625.8 0.6 copy.53
  626.4 0.6 reshape.260
  (35 shorter events, 0.2 us)
Async XLA Ops:
  7.2 148.6 %copy-start = (bf16[8,1024,128]{2,1,0:T(8,128)(2,1)S(1)}, bf16[8,1024,128]{2,1,0:T(8,128)(2,1)}, u32[]{:S(2)}) copy-start(bf16[8,1024,128]{2,1,0:T(8,128)(2,1)} %param.14) | copy-start | bytes 6291460
  7.2 3.1 copy-start.19
  7.2 3.1 copy-start.17
  7.2 3.2 copy-start.11
  7.2 4.0 copy-start.12
  7.2 147.4 %all-reduce.6.cloned.1.call-start = ((), (), s32[]{:S(2)}) async-start(), calls=%async_computation | async-start | bytes 327680 | tf_op jit(solution)/shard_map/psum | solution.py:84
  10.1 587.1 %all-reduce.8.cloned.1.call-start = ((), (), s32[]{:S(2)}) async-start(), calls=%async_computation.1 | async-start | bytes 589824 | tf_op jit(solution)/shard_map/psum | solution.py:112
  10.2 145.6 %copy-start.18 = (f32[64]{0:T(128)}, f32[64]{0:T(128)S(1)}, u32[]{:S(2)}) copy-start(f32[64]{0:T(128)S(1)} %multiply_power_fusion) | copy-start | bytes 772
  10.2 1.7 copy-start.16
  10.3 145.4 %copy-start.13 = (f32[8,5]{1,0:T(8,128)}, f32[8,5]{1,0:T(8,128)S(1)}, u32[]{:S(2)}) copy-start(f32[8,5]{1,0:T(8,128)S(1)} %add_convert_fusion.1) | copy-start | bytes 484
  12.8 143.9 %copy-start.10 = (pred[8,1024]{1,0:T(8,128)(4,1)}, pred[8,1024]{1,0:T(8,128)(4,1)S(1)}, u32[]{:S(2)}) copy-start(pred[8,1024]{1,0:T(8,128)(4,1)S(1)} %get-tuple-element.37) | copy-start | bytes 24580
  12.8 145.1 %copy-start.8 = (pred[8,1024]{1,0:T(8,128)(4,1)}, pred[8,1024]{1,0:T(8,128)(4,1)S(1)}, u32[]{:S(2)}) copy-start(pred[8,1024]{1,0:T(8,128)(4,1)S(1)} %get-tuple-element.38) | copy-start | bytes 24580
  155.7 1.0 copy-start.1
  158.0 1.0 copy-start.5
  271.7 117.8 %copy-start.3 = (f32[8,1,5,8]{3,2,0,1:T(8,128)}, f32[8,1,5,8]{3,2,0,1:T(8,128)S(1)}, u32[]{:S(2)}) copy-start(f32[8,1,5,8]{3,2,0,1:T(8,128)S(1)} %get-tuple-element.19) | copy-start | bytes 3844
  389.4 0.6 copy-start.7
  392.1 3.0 copy-start.6
  392.1 3.0 copy-start.9
  392.1 3.0 copy-start.14
  392.1 3.0 copy-start.20
  395.1 4.4 copy-start.15
  395.1 4.4 copy-start.4
  398.6 200.9 %copy-start.2 = (bf16[1024,256]{1,0:T(8,128)(2,1)S(1)}, bf16[1024,256]{1,0:T(8,128)(2,1)}, u32[]{:S(2)}) copy-start(bf16[1024,256]{1,0:T(8,128)(2,1)} %param.13) | copy-start | bytes 1572868
Sparse Core Ops, SparseCore 0:
  11.5 143.1 all-reduce.5
  398.8 198.3 all-reduce.7
where the time goes:
time: 635 us; the launch traced here: 634 us
  waiting for transfers between devices  339 us (53%)
  blocking collectives  250 us (39%)
  between operations  14.4 us (2%)
  other arithmetic  14.2 us (2%)
  matrix products  11.2 us (2%)
    psum x1, waiting for transfers between devices, per_device(): lax.psum((target_total * factor_target, target_weighted * factor_target[....  197 us
    psum x1, waiting for transfers between devices, per_device(): lax.psum((query_part, key_part, value_part), 'seq')  142 us
    pmax x1, blocking collectives, per_device(): peak_target, peak_draft = lax.pmax((target_peak, draft_peak), 'seq')  113 us
    psum x1, blocking collectives, per_device(): lax.psum((query_part, key_part, value_part), 'seq')  112 us
    psum x1, blocking collectives, per_device(): summed = lax.psum(projected.astype(jnp.bfloat16), 'head')  25.9 us
  transfers between devices with their start and end apart: 2, of which 2 were waited for; matrix products, arithmetic and copies ran while one was open for 1% of the time, Pallas kernels for 0%

commit v1 on v0

v1 whole, which is shorter than its diff:
```python
import jax
import jax.numpy as jnp
import numpy as np
from jax import lax
from jax.experimental import pallas as pl
from jax.experimental.pallas import tpu as pltpu
from jax.sharding import PartitionSpec as P

LANES = 128
ROWS = 8
BATCH = 8
VERIFY = 5
DRAFT = 4
TILES = VERIFY + DRAFT
SEQ = 32
HEADS = 8
TOKENS = BATCH * VERIFY
QUERY_ROWS = TOKENS * ROWS
PER_OWNER = 3
OWNERS = BATCH * TILES // PER_OWNER
MESSAGE = 16
NEGATIVE = -(2.0**100)
SCALE = LANES**-0.5
F32 = jnp.float32
BF16 = jnp.bfloat16


def project(hidden_ref, query_ref, key_ref, value_ref, out_ref, tokens, flat):
    for b in range(BATCH):
        tokens[pl.ds(b * VERIFY, VERIFY), :] = hidden_ref[b].astype(F32)
    rows = tokens[...].astype(BF16)
    query = jnp.dot(rows, query_ref[...], preferred_element_type=F32)
    for h in range(ROWS):
        flat[pl.ds(h, TOKENS, stride=ROWS), :] = query[:, h * LANES : (h + 1) * LANES]
    flat[pl.ds(QUERY_ROWS, TOKENS), :] = jnp.dot(rows, key_ref[...], preferred_element_type=F32)
    flat[pl.ds(QUERY_ROWS + TOKENS, TOKENS), :] = jnp.dot(
        rows, value_ref[...], preferred_element_type=F32
    )
    used = QUERY_ROWS + 2 * TOKENS
    flat[pl.ds(used, SEQ * MESSAGE - used), :] = jnp.zeros((SEQ * MESSAGE - used, LANES), F32)
    out_ref[...] = flat[...].reshape(SEQ, MESSAGE, LANES).astype(out_ref.dtype)


def rotate(parts_ref, cosine_ref, sine_ref, out_ref):
    total = parts_ref[0].astype(F32)
    for s in range(1, SEQ):
        total += parts_ref[s].astype(F32)
    swapped = pltpu.roll(total, LANES // 2, 1)
    rotated = (total * cosine_ref[...] + swapped * sine_ref[...]).astype(BF16)
    for s in range(SEQ):
        out_ref[s] = rotated


def split(value):
    high = value.astype(BF16).astype(F32)
    return high, (value - high).astype(BF16).astype(F32)


def attend(
    lengths_ref, keep_ref, first_ref, all_ref, key_hbm, value_hbm, out_ref, keys, values, sems
):
    def copies(b):
        return (
            pltpu.make_async_copy(key_hbm.at[b], keys.at[b], sems.at[0, b]),
            pltpu.make_async_copy(value_hbm.at[b], values.at[b], sems.at[1, b]),
        )

    for b in range(BATCH):
        for copy in copies(b):
            copy.start()
    context = keys.shape[1]
    first = first_ref[0]
    position = first + lax.broadcasted_iota(jnp.int32, (1, context), 1)
    lane = lax.broadcasted_iota(jnp.int32, (ROWS, LANES), 1)
    new_rows = lax.broadcasted_iota(jnp.int32, (QUERY_ROWS // BATCH, LANES), 0) // ROWS
    new_lanes = lax.broadcasted_iota(jnp.int32, (QUERY_ROWS // BATCH, LANES), 1)
    new_keys = jnp.concatenate(
        [all_ref[pl.ds(QUERY_ROWS, TOKENS), :], jnp.zeros((LANES - TOKENS, LANES), BF16)], axis=0
    )
    new_values = jnp.concatenate(
        [
            all_ref[pl.ds(QUERY_ROWS + TOKENS, TOKENS), :],
            jnp.zeros((LANES - TOKENS, LANES), BF16),
        ],
        axis=0,
    )
    transposed = (((1,), (1,)), ((), ()))
    for b in range(BATCH):
        for copy in copies(b):
            copy.wait()
        query = all_ref[pl.ds(b * VERIFY * ROWS, VERIFY * ROWS), :]
        scores = (
            lax.dot_general(query, keys[b], transposed, preferred_element_type=F32) * SCALE
        )
        new_scores = (
            lax.dot_general(query, new_keys, transposed, preferred_element_type=F32) * SCALE
        )
        new_at = new_lanes - b * VERIFY
        seen = (new_at >= 0) & (new_at <= new_rows) & (first == 0)
        new_scores = jnp.where(seen, new_scores, NEGATIVE)
        live = jnp.where(position < lengths_ref[b], 0.0, NEGATIVE)
        kept = jnp.concatenate(
            [
                jnp.where(
                    keep_ref[b, c] > 0, live[:, c * LANES : (c + 1) * LANES], NEGATIVE
                )
                for c in range(context // LANES)
            ],
            axis=1,
        )
        weighted, stats = [], []
        for bias, rows in ((live, VERIFY * ROWS), (kept, DRAFT * ROWS)):
            masked = scores[:rows] + bias
            masked_new = new_scores[:rows]
            peak = jnp.maximum(
                jnp.max(masked, axis=1, keepdims=True), jnp.max(masked_new, axis=1, keepdims=True)
            )
            peak_high, peak_low = split(peak)
            base = peak_high + peak_low
            weights = jnp.exp(masked - base)
            weights_new = jnp.exp(masked_new - base)
            total = jnp.sum(weights, axis=1, keepdims=True) + jnp.sum(
                weights_new, axis=1, keepdims=True
            )
            result = jnp.dot(weights.astype(BF16), values[b], preferred_element_type=F32)
            result += jnp.dot(weights_new.astype(BF16), new_values, preferred_element_type=F32)
            total_high, total_low = split(total)
            for t in range(rows // ROWS):
                at = slice(t * ROWS, (t + 1) * ROWS)
                weighted.append(result[at])
                stats.append((peak_high[at], peak_low[at], total_high[at], total_low[at]))
        for i in range(TILES // PER_OWNER):
            packed = jnp.zeros((ROWS, LANES), F32)
            for u in range(PER_OWNER):
                for k, value in enumerate(stats[i * PER_OWNER + u]):
                    packed = jnp.where(lane == 4 * u + k, value, packed)
            tiles = weighted[i * PER_OWNER : (i + 1) * PER_OWNER] + [packed]
            out_ref[b * (TILES // PER_OWNER) + i] = jnp.concatenate(tiles, axis=0).astype(BF16)
    for d in range(OWNERS, SEQ):
        out_ref[d] = jnp.zeros(out_ref.shape[1:], BF16)


def merge(parts_ref, out_ref):
    acc_rows = PER_OWNER * ROWS
    stats = []
    for s in range(SEQ):
        packed = parts_ref[s][acc_rows:].astype(F32)
        stats.append(packed + pltpu.roll(packed, LANES - 1, 1))
    peak = stats[0]
    for s in range(1, SEQ):
        peak = jnp.maximum(peak, stats[s])
    total = jnp.zeros((ROWS, LANES), F32)
    sums = [jnp.zeros((ROWS, LANES), F32) for _ in range(PER_OWNER)]
    for s in range(SEQ):
        factor = jnp.exp(stats[s] - peak)
        total += factor * pltpu.roll(stats[s], LANES - 2, 1)
        part = parts_ref[s][:acc_rows].astype(F32)
        for u in range(PER_OWNER):
            sums[u] += part[u * ROWS : (u + 1) * ROWS] * factor[:, 4 * u : 4 * u + 1]
    merged = jnp.concatenate(
        [sums[u] / total[:, 4 * u : 4 * u + 1] for u in range(PER_OWNER)], axis=0
    ).astype(BF16)
    for s in range(SEQ):
        out_ref[s] = merged


def project_out(all_ref, weight_ref, out_ref, attended):
    attended[...] = all_ref[...].astype(F32)
    total = None
    for h in range(ROWS):
        rows = attended[pl.ds(h, BATCH * TILES, stride=ROWS), :].astype(BF16)
        part = jnp.dot(
            rows, weight_ref[h * LANES : (h + 1) * LANES, :], preferred_element_type=F32
        )
        total = part if total is None else total + part
    rounded = total.astype(BF16)
    for h in range(HEADS):
        out_ref[h] = rounded


def add_groups(parts_ref, verify_ref, draft_ref, total):
    summed = parts_ref[0].astype(F32)
    for h in range(1, HEADS):
        summed += parts_ref[h].astype(F32)
    total[...] = summed
    for b in range(BATCH):
        verify_ref[b] = total[pl.ds(b * TILES, VERIFY), :].astype(BF16)
        draft_ref[b] = total[pl.ds(b * TILES + VERIFY, DRAFT), :].astype(BF16)


VMEM = pl.BlockSpec(memory_space=pltpu.VMEM)
SMEM = pl.BlockSpec(memory_space=pltpu.SMEM)
ANY = pl.BlockSpec(memory_space=pl.ANY)


def tables(seq_index, context_lengths):
    at = seq_index * MESSAGE + jnp.arange(MESSAGE, dtype=jnp.int32)
    token = jnp.where(at < QUERY_ROWS, at // ROWS, (at - QUERY_ROWS) % TOKENS)
    plain = at >= QUERY_ROWS + TOKENS
    token = jnp.minimum(token, TOKENS - 1)
    position = context_lengths[token // VERIFY] + token % VERIFY
    half = LANES // 2
    inverse = 500000.0 ** (-(jnp.arange(half, dtype=F32) * 2.0) / LANES)
    angles = position[:, None].astype(F32) * inverse
    cosine, sine = jnp.cos(angles), jnp.sin(angles)
    cosine = jnp.concatenate([cosine, cosine], axis=1)
    sine = jnp.concatenate([-sine, sine], axis=1)
    return jnp.where(plain[:, None], 1.0, cosine), jnp.where(plain[:, None], 0.0, sine)


def exchange(messages, axis):
    return lax.all_to_all(messages, axis, 0, 0, tiled=True)


def per_device(
    hidden_states,
    w_query,
    w_key,
    w_value,
    w_out,
    key_cache,
    value_cache,
    context_lengths,
    keep_blocks,
):
    seq_index = lax.axis_index("seq")
    width = hidden_states.shape[2]
    context = key_cache.shape[1]
    columns = w_out.shape[1]
    shape = jax.ShapeDtypeStruct
    parts = pl.pallas_call(
        project,
        out_shape=shape((SEQ, MESSAGE, LANES), F32),
        in_specs=[VMEM] * 4,
        out_specs=VMEM,
        scratch_shapes=[
            pltpu.VMEM((TOKENS, width), F32),
            pltpu.VMEM((SEQ * MESSAGE, LANES), F32),
        ],
        name="project",
    )(hidden_states, w_query, w_key, w_value)
    cosine, sine = tables(seq_index, context_lengths)
    parts = exchange(parts, "seq")
    rotated = pl.pallas_call(
        rotate,
        out_shape=shape((SEQ, MESSAGE, LANES), BF16),
        in_specs=[VMEM] * 3,
        out_specs=VMEM,
        name="rotate",
    )(parts, cosine, sine)
    rotated = exchange(rotated, "seq")
    first = (seq_index * context).astype(jnp.int32).reshape(1)
    partial = pl.pallas_call(
        attend,
        out_shape=shape((SEQ, (PER_OWNER + 1) * ROWS, LANES), BF16),
        in_specs=[SMEM, SMEM, SMEM, VMEM, ANY, ANY],
        out_specs=VMEM,
        scratch_shapes=[
            pltpu.VMEM((BATCH, context, LANES), BF16),
            pltpu.VMEM((BATCH, context, LANES), BF16),
            pltpu.SemaphoreType.DMA((2, BATCH)),
        ],
        name="attend",
    )(
        context_lengths,
        keep_blocks,
        first,
        rotated.reshape(SEQ * MESSAGE, LANES),
        key_cache,
        value_cache,
    )
    partial = exchange(partial, "seq")
    merged = pl.pallas_call(
        merge,
        out_shape=shape((SEQ, PER_OWNER * ROWS, LANES), BF16),
        in_specs=[VMEM],
        out_specs=VMEM,
        name="merge",
    )(partial)
    merged = exchange(merged, "seq")
    groups = pl.pallas_call(
        project_out,
        out_shape=shape((HEADS, BATCH * TILES, columns), BF16),
        in_specs=[
            pl.BlockSpec((OWNERS * PER_OWNER * ROWS, LANES), lambda i: (0, 0)),
            pl.BlockSpec(w_out.shape, lambda i: (0, 0)),
        ],
        out_specs=pl.BlockSpec((HEADS, BATCH * TILES, columns), lambda i: (0, 0, 0)),
        grid=(1,),
        scratch_shapes=[pltpu.VMEM((BATCH * TILES * ROWS, LANES), F32)],
        name="project_out",
    )(merged.reshape(SEQ * PER_OWNER * ROWS, LANES), w_out)
    groups = exchange(groups, "head")
    return pl.pallas_call(
        add_groups,
        out_shape=(
            shape((BATCH, VERIFY, columns), BF16),
            shape((BATCH, DRAFT, columns), BF16),
        ),
        in_specs=[VMEM],
        out_specs=(VMEM, VMEM),
        scratch_shapes=[pltpu.VMEM((BATCH * TILES, columns), F32)],
        name="add_groups",
    )(groups)


def solution(mesh):
    placed = (
        P(None, None, "seq"),
        P("seq", "head"),
        P("seq", "head"),
        P("seq", "head"),
        P("head", "seq"),
        P(None, "seq", "head"),
        P(None, "seq", "head"),
        P(),
        P(None, "seq"),
    )
    return jax.shard_map(
        per_device,
        mesh=mesh,
        in_specs=placed,
        out_specs=(P(None, None, "seq"), P(None, None, "seq")),
        check_vma=False,
    )
```

time: 635 us -> 106 us (0.17)
  waiting for transfers between devices: 339 us -> 18.4 us
  blocking collectives: 250 us -> 46.5 us
  starting transfers between devices: 0.08 us -> 16.7 us
  Pallas kernels: 0 us -> 16.5 us
  between operations: 14.4 us -> 0.7 us
  other arithmetic: 14.2 us -> 0.89 us
  matrix products: 11.2 us -> 0 us
    psum x2 -> x0, waiting for transfers between devices: 339 us -> none  [the longest x1 197 us: per_device(): lax.psum((target_total * factor_target, target_weighted * factor_target[....]
    psum x2 -> x0, blocking collectives: 138 us -> none  [the longest x1 112 us: per_device(): lax.psum((query_part, key_part, value_part), 'seq')]
    pmax x1 -> x0, blocking collectives: 113 us -> none  [per_device(): peak_target, peak_draft = lax.pmax((target_peak, draft_peak), 'seq')]
    all_to_all x0 -> x3, blocking collectives: none -> 46.5 us  [exchange(): return lax.all_to_all(messages, axis, 0, 0, tiled=True)]
    all_to_all x0 -> x2, waiting for transfers between devices: none -> 18.4 us  [exchange(): return lax.all_to_all(messages, axis, 0, 0, tiled=True)]
    all_to_all x0 -> x2, starting transfers between devices: none -> 16.7 us  [exchange(): return lax.all_to_all(messages, axis, 0, 0, tiled=True)]
    pallas_call x0 -> x6, Pallas kernels: none -> 16.5 us  [the longest x1 7.02 us: per_device(): pl.pallas_call(attend, out_shape=shape((SEQ, (PER_OWNER + 1) * ROWS, LANE...]
    dot_general x10 -> x0, matrix products: 11.2 us -> none  [the longest x2 4.23 us: partial_softmax(): jnp.einsum('bkjgt,btkd->bkjgd', weights.astype(jnp.bfloat16), cache_value...]
  transfers between devices with their start and end apart: 2 -> 2, of which waited for: 2 -> 2; matrix products, arithmetic and copies ran while one was open for 1% -> 2% of each run, Pallas kernels for 0% -> 0%
where the time goes in v1:
time: 106 us; the launch traced here: 105 us
  blocking collectives  46.5 us (44%)
  waiting for transfers between devices  18.4 us (17%)
  starting transfers between devices  16.7 us (16%)
  Pallas kernels  16.5 us (16%)
  local copies, waits for them, and re-layouts  5.38 us (5%)
    all_to_all x3, blocking collectives, exchange(): return lax.all_to_all(messages, axis, 0, 0, tiled=True)  46.5 us
    all_to_all x2, waiting for transfers between devices, exchange(): return lax.all_to_all(messages, axis, 0, 0, tiled=True)  18.4 us
    all_to_all x2, starting transfers between devices, exchange(): return lax.all_to_all(messages, axis, 0, 0, tiled=True)  16.7 us
    pallas_call x1, Pallas kernels, per_device(): pl.pallas_call(attend, out_shape=shape((SEQ, (PER_OWNER + 1) * ROWS, LANE...  7.02 us
    unnamed x5, local copies, waits for them, and re-layouts  2.69 us
  transfers between devices with their start and end apart: 2, of which 2 were waited for; matrix products, arithmetic and copies ran while one was open for 2% of the time, Pallas kernels for 0%

profile of v1, /device:TPU:1, one launch (start us, length us, event | category | flops | bytes accessed | tf_op | source)
XLA Modules:
  0.0 105.1 jit_solution(10598126273386972746)
XLA Ops:
  0.6 1.4 %copy.13.hidden_ref = bf16[8,5,256]{2,1,0:T(8,128)(2,1)} copy(bf16[8,5,256]{2,0,1:T(8,128)(2,1)} %param.9) | data formatting | bytes 40960 | tf_op args[0]
  2.0 2.0 %project.1 = f32[32,16,128]{2,1,0:T(8,128)} custom-call(bf16[8,5,256]{2,1,0:T(8,128)(2,1)} %copy.13.hidden_ref, bf16[256,1024]{1,0:T(8,128)(2,1)} %query_ref.1, bf16[256,128]{1,0:T(8,128)(2,1)} %key_ref.1, bf16[256,128]{1,0:T(8,128)(2,1)} %value_ref.1), custom_call_target="tpu_custom_call" | custom-call | tf_op jit(solution)/shard_map/project/pallas_call | solution.py:231
  4.0 12.0 %all-to-all-start = ((f32[32,16,128]{2,1,0:T(8,128)}), f32[32,16,128]{2,1,0:T(8,128)S(1)}, u32[]{:S(2)}, u32[]{:S(2)}) async-start(f32[32,16,128]{2,1,0:T(8,128)} %project.1), calls=%async_computation | async-start | bytes 524288 | tf_op jit(solution)/shard_map/all_to_all | solution.py:212
  16.1 1.3 %gather_fusion = s32[16]{0:T(128)S(1)} fusion(s32[8]{0:T(128)} %lengths_ref.1, s32[1024]{0:T(1024)S(1)} %pad_clamp_fusion), kind=kCustom, calls=%fused_computation | custom fusion | bytes 192 | tf_op jit(solution)/shard_map/gather | solution.py:201
  17.4 0.1 fusion
  17.6 0.7 maximum_select_fusion.1
  18.2 9.1 %all-to-all-done.parts_ref = f32[32,16,128]{2,1,0:T(8,128)S(1)} async-done(((f32[32,16,128]{2,1,0:T(8,128)}), f32[32,16,128]{2,1,0:T(8,128)S(1)}, u32[]{:S(2)}, u32[]{:S(2)}) %all-to-all-start) | async-done | bytes 262176 | tf_op jit(solution)/shard_map/all_to_all | solution.py:212
  27.3 0.0 copy-start
  27.3 0.7 copy-done
  28.0 1.7 %rotate.1 = bf16[32,16,128]{2,1,0:T(8,128)(2,1)} custom-call(f32[32,16,128]{2,1,0:T(8,128)} %copy-done, f32[16,128]{1,0:T(8,128)} %get-tuple-element.10.cosine_ref, f32[16,128]{1,0:T(8,128)} %get-tuple-element.9.sine_ref), custom_call_target="tpu_custom_call" | custom-call | tf_op jit(solution)/shard_map/rotate/pallas_call | solution.py:244
  29.7 4.7 %all-to-all-start.1 = ((bf16[32,16,128]{2,1,0:T(8,128)(2,1)}), bf16[32,16,128]{2,1,0:T(8,128)(2,1)S(1)}, u32[]{:S(2)}, u32[]{:S(2)}) async-start(bf16[32,16,128]{2,1,0:T(8,128)(2,1)} %rotate.1), calls=%async_computation.1 | async-start | bytes 262144 | tf_op jit(solution)/shard_map/all_to_all | solution.py:212
  34.4 9.3 %all-to-all-done.1 = bf16[32,16,128]{2,1,0:T(8,128)(2,1)S(1)} async-done(((bf16[32,16,128]{2,1,0:T(8,128)(2,1)}), bf16[32,16,128]{2,1,0:T(8,128)(2,1)S(1)}, u32[]{:S(2)}, u32[]{:S(2)}) %all-to-all-start.1) | async-done | bytes 131104 | tf_op jit(solution)/shard_map/all_to_all | solution.py:212
  43.8 0.0 copy-start.1
  43.8 0.6 copy-done.1
  44.4 7.0 %attend.1 = bf16[32,32,128]{2,1,0:T(8,128)(2,1)} custom-call(s32[8]{0:T(128)} %lengths_ref.1, s32[8,8]{1,0:T(8,128)} %keep_ref.1, s32[1]{0:T(128)} %bitcast.first_ref, bf16[512,128]{1,0:T(8,128)(2,1)} %bitcast.6, bf16[8,1024,128]{2,1,0:T(8,128)(2,1)} %key_hbm.1, bf16[8,1024,128]{2,1,0:T(8,128)(2,1)} %value_hbm.1), custom_call_target="tpu_custom_call" | custom-call | tf_op jit(solution)/shard_map/attend/pallas_call | solution.py:253
  51.4 15.2 %all_to_all.25.parts_ref = bf16[32,32,128]{2,1,0:T(8,128)(2,1)} all-to-all(bf16[32,32,128]{2,1,0:T(8,128)(2,1)} %attend.1), channel_id=1, replica_groups=mesh['seq'=32,'head'=8] {'seq'}, dimensions={0} | all-to-all | bytes 524288 | tf_op jit(solution)/shard_map/all_to_all | solution.py:212
  66.6 2.0 %merge.1 = bf16[32,24,128]{2,1,0:T(8,128)(2,1)} custom-call(bf16[32,32,128]{2,1,0:T(8,128)(2,1)} %all_to_all.25.parts_ref), custom_call_target="tpu_custom_call" | custom-call | tf_op jit(solution)/shard_map/merge/pallas_call | solution.py:273
  68.6 14.5 %all_to_all.26 = bf16[32,24,128]{2,1,0:T(8,128)(2,1)} all-to-all(bf16[32,24,128]{2,1,0:T(8,128)(2,1)} %merge.1), channel_id=1, replica_groups=mesh['seq'=32,'head'=8] {'seq'}, dimensions={0} | all-to-all | bytes 393216 | tf_op jit(solution)/shard_map/all_to_all | solution.py:212
  83.1 2.1 %project_out.1 = bf16[8,72,256]{2,1,0:T(8,128)(2,1)} custom-call(bf16[768,128]{1,0:T(8,128)(2,1)} %bitcast.5, bf16[1024,256]{1,0:T(8,128)(2,1)} %weight_ref.1), custom_call_target="tpu_custom_call" | custom-call | tf_op jit(solution)/shard_map/project_out/pallas_call | solution.py:281
  85.2 16.8 %all_to_all.27.parts_ref = bf16[8,72,256]{2,1,0:T(8,128)(2,1)} all-to-all(bf16[8,72,256]{2,1,0:T(8,128)(2,1)} %project_out.1), channel_id=1, replica_groups=mesh['seq'=32,'head'=8] {'head'}, dimensions={0} | all-to-all | bytes 589824 | tf_op jit(solution)/shard_map/all_to_all | solution.py:212
  102.1 1.6 %add_groups.1 = (bf16[8,5,256]{2,1,0:T(8,128)(2,1)}, bf16[8,4,256]{2,1,0:T(4,128)(2,1)}) custom-call(bf16[8,72,256]{2,1,0:T(8,128)(2,1)} %all_to_all.27.parts_ref), custom_call_target="tpu_custom_call" | custom-call | tf_op jit(solution)/shard_map/add_groups/pallas_call | solution.py:294
  103.7 1.4 %copy.14 = bf16[8,5,256]{2,0,1:T(8,128)(2,1)} copy(bf16[8,5,256]{2,1,0:T(8,128)(2,1)} %get-tuple-element.4) | data formatting | bytes 40960 | tf_op jit(solution)/shard_map/add_groups/pallas_call | solution.py:294
  (5 shorter events, 0.1 us)
Async XLA Ops:
  4.0 23.3 %all-to-all-start = ((f32[32,16,128]{2,1,0:T(8,128)}), f32[32,16,128]{2,1,0:T(8,128)S(1)}, u32[]{:S(2)}, u32[]{:S(2)}) async-start(f32[32,16,128]{2,1,0:T(8,128)} %project.1), calls=%async_computation | async-start | bytes 524288 | tf_op jit(solution)/shard_map/all_to_all | solution.py:212
  27.3 0.7 copy-start
  29.7 14.1 %all-to-all-start.1 = ((bf16[32,16,128]{2,1,0:T(8,128)(2,1)}), bf16[32,16,128]{2,1,0:T(8,128)(2,1)S(1)}, u32[]{:S(2)}, u32[]{:S(2)}) async-start(bf16[32,16,128]{2,1,0:T(8,128)(2,1)} %rotate.1), calls=%async_computation.1 | async-start | bytes 262144 | tf_op jit(solution)/shard_map/all_to_all | solution.py:212
  43.8 0.6 copy-start.1

commit v2 on v1

v2 whole, which is shorter than its diff:
```python
import jax
import jax.numpy as jnp
import numpy as np
from jax import lax
from jax.experimental import pallas as pl
from jax.experimental.pallas import tpu as pltpu
from jax.sharding import PartitionSpec as P

LANES = 128
ROWS = 8
BATCH = 8
VERIFY = 5
DRAFT = 4
TILES = VERIFY + DRAFT
SEQ = 32
HEADS = 8
TOKENS = BATCH * VERIFY
QUERY_ROWS = TOKENS * ROWS
PER_OWNER = 3
OWNERS = BATCH * TILES // PER_OWNER
MESSAGE = 16
NEGATIVE = -(2.0**100)
SCALE = LANES**-0.5
LOG2E = float(np.log2(np.e))
F32 = jnp.float32
BF16 = jnp.bfloat16


def project(
    hidden_hbm, query_hbm, key_hbm, value_hbm, out_ref,
    hidden_ref, query_ref, key_ref, value_ref, flat, sems,
):
    pairs = (
        (hidden_hbm, hidden_ref),
        (query_hbm, query_ref),
        (key_hbm, key_ref),
        (value_hbm, value_ref),
    )
    loads = [
        pltpu.make_async_copy(source, target, sems.at[i])
        for i, (source, target) in enumerate(pairs)
    ]
    for load in loads:
        load.start()
    for load in loads:
        load.wait()
    rows = hidden_ref[...]
    query = jnp.dot(rows, query_ref[...], preferred_element_type=F32)
    for h in range(ROWS):
        flat[pl.ds(h, TOKENS, stride=ROWS), :] = query[:, h * LANES : (h + 1) * LANES]
    flat[pl.ds(QUERY_ROWS, TOKENS), :] = jnp.dot(rows, key_ref[...], preferred_element_type=F32)
    flat[pl.ds(QUERY_ROWS + TOKENS, TOKENS), :] = jnp.dot(
        rows, value_ref[...], preferred_element_type=F32
    )
    used = QUERY_ROWS + 2 * TOKENS
    flat[pl.ds(used, SEQ * MESSAGE - used), :] = jnp.zeros((SEQ * MESSAGE - used, LANES), F32)
    out_ref[...] = flat[...].reshape(SEQ, MESSAGE, LANES).astype(out_ref.dtype)


def rotate(parts_ref, cosine_ref, sine_ref, out_ref):
    total = parts_ref[0].astype(F32)
    for s in range(1, SEQ):
        total += parts_ref[s].astype(F32)
    swapped = pltpu.roll(total, LANES // 2, 1)
    rotated = (total * cosine_ref[...] + swapped * sine_ref[...]).astype(BF16)
    for s in range(SEQ):
        out_ref[s] = rotated


def split(value):
    high = value.astype(BF16).astype(F32)
    return high, (value - high).astype(BF16).astype(F32)


def attend(
    lengths_ref, keep_ref, first_ref, all_ref, keys, value_hbm, out_ref, scores, weights, values, sem
):
    load_values = pltpu.make_async_copy(value_hbm, values, sem)
    load_values.start()
    context = keys.shape[1]
    blocks = context // LANES
    first = first_ref[0]
    position = first + lax.broadcasted_iota(jnp.int32, (1, context), 1)
    lane = lax.broadcasted_iota(jnp.int32, (ROWS, LANES), 1)
    lane_row = lax.rem(lane, BATCH)
    padding = jnp.zeros((LANES - TOKENS, LANES), BF16)
    new_keys = jnp.concatenate([all_ref[pl.ds(QUERY_ROWS, TOKENS), :], padding], axis=0)
    new_values = jnp.concatenate([all_ref[pl.ds(QUERY_ROWS + TOKENS, TOKENS), :], padding], axis=0)
    transposed = (((1,), (1,)), ((), ()))
    exponent = SCALE * LOG2E

    def tile(j, b):
        return pl.ds((j * BATCH + b) * ROWS, ROWS)

    new_scores = (
        lax.dot_general(
            all_ref[pl.ds(0, QUERY_ROWS), :], new_keys, transposed, preferred_element_type=F32
        )
        * exponent
    )
    for b in range(BATCH):
        query = jnp.concatenate([all_ref[tile(j, b), :] for j in range(VERIFY)], axis=0)
        live = jnp.where(position < lengths_ref[b], 0.0, NEGATIVE)
        scores[b] = (
            lax.dot_general(query, keys[b], transposed, preferred_element_type=F32) * exponent
            + live
        )
    kept, fresh, bases = [], [], []
    for b in range(BATCH):
        kept.append([jnp.where(keep_ref[b, c] > 0, 0.0, NEGATIVE) for c in range(blocks)])
        rows = []
        for j in range(VERIFY):
            at = (j * BATCH + b) * ROWS
            limit = jnp.where(first == 0, (j + 1) * BATCH, 0)
            seen = (lane_row == b) & (lane < limit)
            rows.append(jnp.where(seen, new_scores[at : at + ROWS], NEGATIVE))
        rows = jnp.concatenate(rows, axis=0)
        target, draft = rows, rows[: DRAFT * ROWS]
        fresh.append(jnp.concatenate([target, draft], axis=0))
        for c in range(blocks):
            block = scores[b, :, c * LANES : (c + 1) * LANES]
            target = jnp.maximum(target, block)
            draft = jnp.maximum(draft, block[: DRAFT * ROWS] + kept[b][c])
        peak = jnp.max(jnp.concatenate([target, draft], axis=0), axis=1, keepdims=True)
        bases.append(split(peak))
    totals, fresh_weights = [], []
    for b in range(BATCH):
        base = bases[b][0] + bases[b][1]
        base_target = base[: VERIFY * ROWS]
        base_draft = base[VERIFY * ROWS :]
        new_weights = jnp.exp2(fresh[b] - base)
        fresh_weights.append(new_weights)
        sums = new_weights
        for c in range(blocks):
            at = slice(c * LANES, (c + 1) * LANES)
            block = scores[b, :, at]
            result = jnp.concatenate(
                [
                    jnp.exp2(block - base_target),
                    jnp.exp2(block[: DRAFT * ROWS] + kept[b][c] - base_draft),
                ],
                axis=0,
            )
            sums += result
            weights[b, :, at] = result.astype(BF16)
        totals.append(jnp.sum(sums, axis=1, keepdims=True))
    fresh_result = jnp.dot(
        jnp.concatenate(fresh_weights, axis=0).astype(BF16),
        new_values,
        preferred_element_type=F32,
    )
    rows = TILES * ROWS
    load_values.wait()
    for b in range(BATCH):
        result = jnp.dot(weights[b], values[b], preferred_element_type=F32)
        result += fresh_result[b * rows : (b + 1) * rows]
        stats = bases[b] + split(totals[b])
        for i in range(TILES // PER_OWNER):
            packed = jnp.zeros((ROWS, LANES), F32)
            for u in range(PER_OWNER):
                t = i * PER_OWNER + u
                for k, value in enumerate(stats):
                    packed = jnp.where(
                        lane == 4 * u + k, value[t * ROWS : (t + 1) * ROWS], packed
                    )
            part = result[i * PER_OWNER * ROWS : (i + 1) * PER_OWNER * ROWS]
            out_ref[b * (TILES // PER_OWNER) + i] = jnp.concatenate([part, packed], axis=0).astype(
                BF16
            )
    for d in range(OWNERS, SEQ):
        out_ref[d] = jnp.zeros(out_ref.shape[1:], BF16)


def merge(parts_ref, out_ref):
    acc_rows = PER_OWNER * ROWS
    stats = []
    for s in range(SEQ):
        packed = parts_ref[s][acc_rows:].astype(F32)
        stats.append(packed + pltpu.roll(packed, LANES - 1, 1))
    peak = stats[0]
    for s in range(1, SEQ):
        peak = jnp.maximum(peak, stats[s])
    total = jnp.zeros((ROWS, LANES), F32)
    sums = [jnp.zeros((ROWS, LANES), F32) for _ in range(PER_OWNER)]
    for s in range(SEQ):
        factor = jnp.exp2(stats[s] - peak)
        total += factor * pltpu.roll(stats[s], LANES - 2, 1)
        part = parts_ref[s][:acc_rows].astype(F32)
        for u in range(PER_OWNER):
            sums[u] += part[u * ROWS : (u + 1) * ROWS] * factor[:, 4 * u : 4 * u + 1]
    merged = jnp.concatenate(
        [sums[u] / total[:, 4 * u : 4 * u + 1] for u in range(PER_OWNER)], axis=0
    ).astype(BF16)
    for s in range(SEQ):
        out_ref[s] = merged


def project_out(all_ref, weight_ref, out_ref, attended):
    attended[...] = all_ref[pl.ds(0, BATCH * TILES * ROWS), :].astype(F32)
    total = None
    for h in range(ROWS):
        rows = jnp.concatenate(
            [attended[pl.ds(t * ROWS + h, BATCH, stride=TILES * ROWS), :] for t in range(TILES)],
            axis=0,
        ).astype(BF16)
        part = jnp.dot(
            rows, weight_ref[h * LANES : (h + 1) * LANES, :], preferred_element_type=F32
        )
        total = part if total is None else total + part
    rounded = total.astype(BF16)
    for h in range(HEADS):
        out_ref[h] = rounded


def add_groups(parts_ref, verify_ref, draft_ref, *halves):
    summed = parts_ref[0].astype(F32)
    for h in range(1, HEADS):
        summed += parts_ref[h].astype(F32)
    rounded = summed.astype(BF16)
    for j in range(VERIFY):
        verify_ref[j] = rounded[j * BATCH : (j + 1) * BATCH]
    for k, half in enumerate(halves):
        at = slice(k * LANES, (k + 1) * LANES)
        half[...] = summed[TOKENS:, at]
        for b in range(BATCH):
            draft_ref[b, :, at] = half[pl.ds(b, DRAFT, stride=BATCH), :].astype(BF16)


VMEM = pl.BlockSpec(memory_space=pltpu.VMEM)
SMEM = pl.BlockSpec(memory_space=pltpu.SMEM)
HBM = pl.BlockSpec(memory_space=pltpu.HBM)


def resident(array):
    return pltpu.with_memory_space_constraint(array, pltpu.VMEM)


def in_place(array):
    return pltpu.with_memory_space_constraint(array, pltpu.HBM)


def tables(seq_index, context_lengths):
    at = seq_index * MESSAGE + jnp.arange(MESSAGE, dtype=jnp.int32)
    token = jnp.where(at < QUERY_ROWS, at // ROWS, (at - QUERY_ROWS) % TOKENS)
    plain = at >= QUERY_ROWS + TOKENS
    token = jnp.minimum(token, TOKENS - 1)
    position = context_lengths[token % BATCH] + token // BATCH
    half = LANES // 2
    inverse = 500000.0 ** (-(jnp.arange(half, dtype=F32) * 2.0) / LANES)
    angles = position[:, None].astype(F32) * inverse
    cosine, sine = jnp.cos(angles), jnp.sin(angles)
    cosine = jnp.concatenate([cosine, cosine], axis=1)
    sine = jnp.concatenate([-sine, sine], axis=1)
    return jnp.where(plain[:, None], 1.0, cosine), jnp.where(plain[:, None], 0.0, sine)


def exchange(messages, axis):
    return lax.all_to_all(messages, axis, 0, 0, tiled=True)


def per_device(
    hidden_states,
    w_query,
    w_key,
    w_value,
    w_out,
    key_cache,
    value_cache,
    context_lengths,
    keep_blocks,
):
    seq_index = lax.axis_index("seq")
    width = hidden_states.shape[2]
    context = key_cache.shape[1]
    columns = w_out.shape[1]
    rows = hidden_states.transpose(1, 0, 2).reshape(TOKENS, width)
    parts = pl.pallas_call(
        project,
        out_shape=pltpu.VMEM((SEQ, MESSAGE, LANES), BF16),
        in_specs=[HBM] * 4,
        out_specs=VMEM,
        scratch_shapes=[
            pltpu.VMEM((TOKENS, width), BF16),
            pltpu.VMEM(w_query.shape, BF16),
            pltpu.VMEM(w_key.shape, BF16),
            pltpu.VMEM(w_value.shape, BF16),
            pltpu.VMEM((SEQ * MESSAGE, LANES), F32),
            pltpu.SemaphoreType.DMA((4,)),
        ],
        name="project",
        compiler_params=pltpu.CompilerParams(vmem_limit_bytes=8 << 20),
    )(*(in_place(array) for array in (rows, w_query, w_key, w_value)))
    cosine, sine = tables(seq_index, context_lengths)
    parts = exchange(parts, "seq")
    rotated = pl.pallas_call(
        rotate,
        out_shape=pltpu.VMEM((SEQ, MESSAGE, LANES), BF16),
        in_specs=[VMEM] * 3,
        out_specs=VMEM,
        name="rotate",
        compiler_params=pltpu.CompilerParams(vmem_limit_bytes=8 << 20),
    )(resident(parts), resident(cosine), resident(sine))
    rotated = exchange(rotated, "seq")
    first = (seq_index * context).astype(jnp.int32).reshape(1)
    partial = pl.pallas_call(
        attend,
        out_shape=pltpu.VMEM((SEQ, (PER_OWNER + 1) * ROWS, LANES), BF16),
        in_specs=[SMEM, SMEM, SMEM, VMEM, VMEM, HBM],
        out_specs=VMEM,
        scratch_shapes=[
            pltpu.VMEM((BATCH, VERIFY * ROWS, context), F32),
            pltpu.VMEM((BATCH, TILES * ROWS, context), BF16),
            pltpu.VMEM((BATCH, context, LANES), BF16),
            pltpu.SemaphoreType.DMA,
        ],
        name="attend",
        compiler_params=pltpu.CompilerParams(vmem_limit_bytes=16 << 20),
    )(
        context_lengths,
        keep_blocks,
        first,
        resident(rotated.reshape(SEQ * MESSAGE, LANES)),
        resident(key_cache),
        in_place(value_cache),
    )
    partial = exchange(partial, "seq")
    merged = pl.pallas_call(
        merge,
        out_shape=pltpu.VMEM((SEQ, PER_OWNER * ROWS, LANES), BF16),
        in_specs=[VMEM],
        out_specs=VMEM,
        name="merge",
        compiler_params=pltpu.CompilerParams(vmem_limit_bytes=8 << 20),
    )(resident(partial))
    merged = exchange(merged, "seq").reshape(SEQ * PER_OWNER * ROWS, LANES)
    groups = pl.pallas_call(
        project_out,
        out_shape=pltpu.VMEM((HEADS, BATCH * TILES, columns), BF16),
        in_specs=[VMEM, VMEM],
        out_specs=VMEM,
        scratch_shapes=[pltpu.VMEM((BATCH * TILES * ROWS, LANES), F32)],
        name="project_out",
        compiler_params=pltpu.CompilerParams(vmem_limit_bytes=8 << 20),
    )(resident(merged), resident(w_out))
    groups = exchange(groups, "head")
    verify_out, draft_out = pl.pallas_call(
        add_groups,
        out_shape=(
            jax.ShapeDtypeStruct((VERIFY, BATCH, columns), BF16),
            jax.ShapeDtypeStruct((BATCH, DRAFT, columns), BF16),
        ),
        in_specs=[VMEM],
        out_specs=(VMEM, VMEM),
        scratch_shapes=[pltpu.VMEM((DRAFT * BATCH, LANES), F32)] * (columns // LANES),
        name="add_groups",
        compiler_params=pltpu.CompilerParams(vmem_limit_bytes=8 << 20),
    )(resident(groups))
    return verify_out.transpose(1, 0, 2), draft_out


def solution(mesh):
    placed = (
        P(None, None, "seq"),
        P("seq", "head"),
        P("seq", "head"),
        P("seq", "head"),
        P("head", "seq"),
        P(None, "seq", "head"),
        P(None, "seq", "head"),
        P(),
        P(None, "seq"),
    )
    return jax.shard_map(
        per_device,
        mesh=mesh,
        in_specs=placed,
        out_specs=(P(None, None, "seq"), P(None, None, "seq")),
        check_vma=False,
    )
```

time: 106 us -> 87 us (0.82)
  Pallas kernels: 16.5 us -> 7.36 us
  local copies, waits for them, and re-layouts: 5.38 us -> 1.34 us
  blocking collectives: 46.5 us -> 43.9 us
  waiting for transfers between devices: 18.4 us -> 17.1 us
    pallas_call x6, Pallas kernels: 16.5 us -> 7.36 us  [the longest x1 3.16 us: per_device(): pl.pallas_call(attend, out_shape=pltpu.VMEM((SEQ, (PER_OWNER + 1) * ROWS,...]
    unnamed x5 -> x8, local copies, waits for them, and re-layouts: 2.69 us -> 0.02 us
    all_to_all x3, blocking collectives: 46.5 us -> 43.9 us  [exchange(): return lax.all_to_all(messages, axis, 0, 0, tiled=True)]
    pallas_call x1 -> x0, local copies, waits for them, and re-layouts: 1.37 us -> none  [per_device(): pl.pallas_call(add_groups, out_shape=(shape((BATCH, VERIFY, columns), BF1...]
    all_to_all x2, waiting for transfers between devices: 18.4 us -> 17.1 us  [exchange(): return lax.all_to_all(messages, axis, 0, 0, tiled=True)]
where the time goes in v2:
time: 87 us; the launch traced here: 86.6 us
  blocking collectives  43.9 us (50%)
  waiting for transfers between devices  17.1 us (20%)
  starting transfers between devices  15.9 us (18%)
  Pallas kernels  7.36 us (8%)
  local copies, waits for them, and re-layouts  1.34 us (2%)
    all_to_all x3, blocking collectives, exchange(): return lax.all_to_all(messages, axis, 0, 0, tiled=True)  43.9 us
    all_to_all x2, waiting for transfers between devices, exchange(): return lax.all_to_all(messages, axis, 0, 0, tiled=True)  17.1 us
    all_to_all x2, starting transfers between devices, exchange(): return lax.all_to_all(messages, axis, 0, 0, tiled=True)  15.9 us
    pallas_call x1, Pallas kernels, per_device(): pl.pallas_call(attend, out_shape=pltpu.VMEM((SEQ, (PER_OWNER + 1) * ROWS,...  3.16 us
    pallas_call x1, Pallas kernels, per_device(): pl.pallas_call(project, out_shape=pltpu.VMEM((SEQ, MESSAGE, LANES), BF16)...  2.12 us
  transfers between devices with their start and end apart: 2, of which 2 were waited for; matrix products, arithmetic and copies ran while one was open for 2% of the time, Pallas kernels for 0%

profile of v2, /device:TPU:1, one launch (start us, length us, event | category | flops | bytes accessed | tf_op | source)
XLA Modules:
  0.0 86.6 jit_solution(6370116497788040620)
XLA Ops:
  0.6 0.0 copy-start
  0.6 0.0 copy-start.3
  0.7 0.0 copy-start.1
  0.7 2.1 %project.1 = bf16[32,16,128]{2,1,0:T(8,128)(2,1)} custom-call(bf16[40,256]{1,0:T(8,128)(2,1)} %bitcast.11, bf16[256,1024]{1,0:T(8,128)(2,1)} %query_hbm.1, bf16[256,128]{1,0:T(8,128)(2,1)} %key_hbm.1, bf16[256,128]{1,0:T(8,128)(2,1)} %value_hbm.2), custom_call_target="tpu_custom_call" | custom-call | tf_op jit(solution)/shard_map/project/pallas_call | solution.py:277
  2.8 12.0 %all-to-all-start = ((bf16[32,16,128]{2,1,0:T(8,128)(2,1)}), bf16[32,16,128]{2,1,0:T(8,128)(2,1)S(1)}, u32[]{:S(2)}, u32[]{:S(2)}) async-start(bf16[32,16,128]{2,1,0:T(8,128)(2,1)} %project.1), calls=%async_computation | async-start | bytes 262144 | tf_op jit(solution)/shard_map/all_to_all | solution.py:258
  14.9 1.3 %gather_fusion = s32[16]{0:T(128)S(1)} fusion(s32[8]{0:T(128)} %lengths_ref.1, s32[1024]{0:T(1024)S(1)} %pad_clamp_fusion), kind=kCustom, calls=%fused_computation | custom fusion | bytes 192 | tf_op jit(solution)/shard_map/gather | solution.py:247
  16.3 0.1 fusion
  16.4 0.1 maximum_select_fusion.1
  16.5 7.7 %all-to-all-done.parts_ref = bf16[32,16,128]{2,1,0:T(8,128)(2,1)S(1)} async-done(((bf16[32,16,128]{2,1,0:T(8,128)(2,1)}), bf16[32,16,128]{2,1,0:T(8,128)(2,1)S(1)}, u32[]{:S(2)}, u32[]{:S(2)}) %all-to-all-start) | async-done | bytes 131104 | tf_op jit(solution)/shard_map/all_to_all | solution.py:258
  24.2 0.8 rotate.1
  24.9 3.9 %all-to-all-start.1 = ((bf16[32,16,128]{2,1,0:T(8,128)(2,1)}), bf16[32,16,128]{2,1,0:T(8,128)(2,1)S(1)}, u32[]{:S(2)}, u32[]{:S(2)}) async-start(bf16[32,16,128]{2,1,0:T(8,128)(2,1)} %rotate.1), calls=%async_computation.1 | async-start | bytes 262144 | tf_op jit(solution)/shard_map/all_to_all | solution.py:258
  28.8 9.4 %all-to-all-done.1 = bf16[32,16,128]{2,1,0:T(8,128)(2,1)S(1)} async-done(((bf16[32,16,128]{2,1,0:T(8,128)(2,1)}), bf16[32,16,128]{2,1,0:T(8,128)(2,1)S(1)}, u32[]{:S(2)}, u32[]{:S(2)}) %all-to-all-start.1) | async-done | bytes 131104 | tf_op jit(solution)/shard_map/all_to_all | solution.py:258
  38.2 0.0 copy-done
  38.2 0.0 copy-done.3
  38.2 0.0 copy-done.1
  38.2 0.0 copy-start.2
  38.2 3.2 %attend.1 = bf16[32,32,128]{2,1,0:T(8,128)(2,1)S(1)} custom-call(s32[8]{0:T(128)S(1)} %copy-done, s32[8,8]{1,0:T(8,128)S(1)} %copy-done.3, s32[1]{0:T(128)} %bitcast.first_ref, bf16[512,128]{1,0:T(8,128)(2,1)S(1)} %bitcast.10, bf16[8,1024,128]{2,1,0:T(8,128)(2,1)S(1)} %copy-done.1, bf16[8,1024,128]{2,1,0:T(8,128)(2,1)} %value_hbm.3), custom_call_target="tpu_custom_call" | custom-call | tf_op jit(solution)/shard_map/attend/pallas_call | solution.py:305
  41.4 13.6 %all_to_all.25.parts_ref = bf16[32,32,128]{2,1,0:T(8,128)(2,1)S(1)} all-to-all(bf16[32,32,128]{2,1,0:T(8,128)(2,1)S(1)} %attend.1), channel_id=1, replica_groups=mesh['seq'=32,'head'=8] {'seq'}, dimensions={0} | all-to-all | bytes 524288 | tf_op jit(solution)/shard_map/all_to_all | solution.py:258
  55.0 0.4 merge.1
  55.4 13.5 %all_to_all.26 = bf16[32,24,128]{2,1,0:T(8,128)(2,1)S(1)} all-to-all(bf16[32,24,128]{2,1,0:T(8,128)(2,1)S(1)} %merge.1), channel_id=1, replica_groups=mesh['seq'=32,'head'=8] {'seq'}, dimensions={0} | all-to-all | bytes 393216 | tf_op jit(solution)/shard_map/all_to_all | solution.py:258
  68.9 0.0 copy-done.2
  68.9 0.3 project_out.1
  69.2 16.8 %all_to_all.27.parts_ref = bf16[8,72,256]{2,1,0:T(8,128)(2,1)S(1)} all-to-all(bf16[8,72,256]{2,1,0:T(8,128)(2,1)S(1)} %project_out.1), channel_id=1, replica_groups=mesh['seq'=32,'head'=8] {'head'}, dimensions={0} | all-to-all | bytes 589824 | tf_op jit(solution)/shard_map/all_to_all | solution.py:258
  86.0 0.7 add_groups.1
  (5 shorter events, 0.1 us)
Async XLA Ops:
  0.6 37.6 %copy-start = (s32[8]{0:T(128)S(1)}, s32[8]{0:T(128)}, u32[]{:S(2)}) copy-start(s32[8]{0:T(128)} %lengths_ref.1) | copy-start | bytes 100
  0.6 37.6 %copy-start.3 = (s32[8,8]{1,0:T(8,128)S(1)}, s32[8,8]{1,0:T(8,128)}, u32[]{:S(2)}) copy-start(s32[8,8]{1,0:T(8,128)} %keep_ref.1) | copy-start | bytes 772
  0.7 37.6 %copy-start.1 = (bf16[8,1024,128]{2,1,0:T(8,128)(2,1)S(1)}, bf16[8,1024,128]{2,1,0:T(8,128)(2,1)}, u32[]{:S(2)}) copy-start(bf16[8,1024,128]{2,1,0:T(8,128)(2,1)} %keys.1) | copy-start | bytes 6291460
  2.8 21.4 %all-to-all-start = ((bf16[32,16,128]{2,1,0:T(8,128)(2,1)}), bf16[32,16,128]{2,1,0:T(8,128)(2,1)S(1)}, u32[]{:S(2)}, u32[]{:S(2)}) async-start(bf16[32,16,128]{2,1,0:T(8,128)(2,1)} %project.1), calls=%async_computation | async-start | bytes 262144 | tf_op jit(solution)/shard_map/all_to_all | solution.py:258
  24.9 13.3 %all-to-all-start.1 = ((bf16[32,16,128]{2,1,0:T(8,128)(2,1)}), bf16[32,16,128]{2,1,0:T(8,128)(2,1)S(1)}, u32[]{:S(2)}, u32[]{:S(2)}) async-start(bf16[32,16,128]{2,1,0:T(8,128)(2,1)} %rotate.1), calls=%async_computation.1 | async-start | bytes 262144 | tf_op jit(solution)/shard_map/all_to_all | solution.py:258
  38.2 30.7 %copy-start.2 = (bf16[1024,256]{1,0:T(8,128)(2,1)S(1)}, bf16[1024,256]{1,0:T(8,128)(2,1)}, u32[]{:S(2)}) copy-start(bf16[1024,256]{1,0:T(8,128)(2,1)} %weight_ref.1) | copy-start | bytes 1572868

commit v3 on v2

--- a/solution.py
+++ b/solution.py
@@ -27,10 +27,14 @@
 
 
 def project(
-    hidden_hbm, query_hbm, key_hbm, value_hbm, out_ref,
-    hidden_ref, query_ref, key_ref, value_ref, flat, sems,
+    hidden_hbm, query_hbm, key_hbm, value_hbm, lengths_hbm, keep_hbm, inverse_hbm,
+    out_ref, cosine_ref, sine_ref, live_ref, kept_ref, fresh_ref,
+    hidden_ref, query_ref, key_ref, value_ref, lengths_ref, keep_ref, inverse_ref, flat, sems,
 ):
     pairs = (
+        (lengths_hbm, lengths_ref),
+        (keep_hbm, keep_ref),
+        (inverse_hbm, inverse_ref),
         (hidden_hbm, hidden_ref),
         (query_hbm, query_ref),
         (key_hbm, key_ref),
@@ -42,7 +46,37 @@
     ]
     for load in loads:
         load.start()
-    for load in loads:
+    for load in loads[:3]:
+        load.wait()
+    here = lax.axis_index("seq")
+    row = lax.broadcasted_iota(jnp.int32, (ROWS, LANES), 0)
+    lane = lax.broadcasted_iota(jnp.int32, (ROWS, LANES), 1)
+    lengths = jnp.zeros((ROWS, LANES), jnp.int32)
+    for b in range(BATCH):
+        lengths = jnp.where(row == b, lengths_ref[b], lengths)
+    for half in range(MESSAGE // ROWS):
+        tile = here * (MESSAGE // ROWS) + half
+        is_query = tile < TOKENS
+        token = jnp.where(is_query, tile, 0)
+        query_position = lengths_ref[lax.rem(token, BATCH)] + token // BATCH
+        position = jnp.where(is_query, query_position, lengths + (tile - TOKENS))
+        angle = position.astype(F32) * inverse_ref[...]
+        plain = tile >= TOKENS + VERIFY
+        at = slice(half * ROWS, (half + 1) * ROWS)
+        sine = jnp.sin(angle)
+        cosine_ref[at, :] = jnp.where(plain, 1.0, jnp.cos(angle))
+        sine_ref[at, :] = jnp.where(plain, 0.0, jnp.where(lane < LANES // 2, -sine, sine))
+    blocks = live_ref.shape[1] // LANES
+    for c in range(blocks):
+        at = slice(c * LANES, (c + 1) * LANES)
+        live = jnp.where((here * blocks + c) * LANES + lane < lengths, 0.0, NEGATIVE)
+        live_ref[:, at] = live
+        keep = jnp.zeros((ROWS, LANES), jnp.int32)
+        for b in range(BATCH):
+            keep = jnp.where(row == b, keep_ref[b, c], keep)
+        kept_ref[:, at] = jnp.where(keep > 0, 0.0, NEGATIVE)
+    fresh_ref[...] = jnp.full((ROWS, LANES), jnp.where(here == 0, 0.0, NEGATIVE))
+    for load in loads[3:]:
         load.wait()
     rows = hidden_ref[...]
     query = jnp.dot(rows, query_ref[...], preferred_element_type=F32)
@@ -73,14 +107,9 @@
 
 
 def attend(
-    lengths_ref, keep_ref, first_ref, all_ref, keys, value_hbm, out_ref, scores, weights, values, sem
+    live_ref, kept_ref, fresh_ref, all_ref, keys, values, out_ref, scores, weights
 ):
-    load_values = pltpu.make_async_copy(value_hbm, values, sem)
-    load_values.start()
-    context = keys.shape[1]
-    blocks = context // LANES
-    first = first_ref[0]
-    position = first + lax.broadcasted_iota(jnp.int32, (1, context), 1)
+    blocks = keys.shape[1] // LANES
     lane = lax.broadcasted_iota(jnp.int32, (ROWS, LANES), 1)
     lane_row = lax.rem(lane, BATCH)
     padding = jnp.zeros((LANES - TOKENS, LANES), BF16)
@@ -100,20 +129,18 @@
     )
     for b in range(BATCH):
         query = jnp.concatenate([all_ref[tile(j, b), :] for j in range(VERIFY)], axis=0)
-        live = jnp.where(position < lengths_ref[b], 0.0, NEGATIVE)
         scores[b] = (
             lax.dot_general(query, keys[b], transposed, preferred_element_type=F32) * exponent
-            + live
+            + live_ref[b : b + 1, :]
         )
     kept, fresh, bases = [], [], []
     for b in range(BATCH):
-        kept.append([jnp.where(keep_ref[b, c] > 0, 0.0, NEGATIVE) for c in range(blocks)])
+        kept.append([kept_ref[b : b + 1, c * LANES : (c + 1) * LANES] for c in range(blocks)])
         rows = []
         for j in range(VERIFY):
             at = (j * BATCH + b) * ROWS
-            limit = jnp.where(first == 0, (j + 1) * BATCH, 0)
-            seen = (lane_row == b) & (lane < limit)
-            rows.append(jnp.where(seen, new_scores[at : at + ROWS], NEGATIVE))
+            seen = (lane_row == b) & (lane < (j + 1) * BATCH)
+            rows.append(jnp.where(seen, new_scores[at : at + ROWS] + fresh_ref[...], NEGATIVE))
         rows = jnp.concatenate(rows, axis=0)
         target, draft = rows, rows[: DRAFT * ROWS]
         fresh.append(jnp.concatenate([target, draft], axis=0))
@@ -150,7 +177,6 @@
         preferred_element_type=F32,
     )
     rows = TILES * ROWS
-    load_values.wait()
     for b in range(BATCH):
         result = jnp.dot(weights[b], values[b], preferred_element_type=F32)
         result += fresh_result[b * rows : (b + 1) * rows]
@@ -227,7 +253,6 @@
 
 
 VMEM = pl.BlockSpec(memory_space=pltpu.VMEM)
-SMEM = pl.BlockSpec(memory_space=pltpu.SMEM)
 HBM = pl.BlockSpec(memory_space=pltpu.HBM)
 
 
@@ -237,21 +262,6 @@
 
 def in_place(array):
     return pltpu.with_memory_space_constraint(array, pltpu.HBM)
-
-
-def tables(seq_index, context_lengths):
-    at = seq_index * MESSAGE + jnp.arange(MESSAGE, dtype=jnp.int32)
-    token = jnp.where(at < QUERY_ROWS, at // ROWS, (at - QUERY_ROWS) % TOKENS)
-    plain = at >= QUERY_ROWS + TOKENS
-    token = jnp.minimum(token, TOKENS - 1)
-    position = context_lengths[token % BATCH] + token // BATCH
-    half = LANES // 2
-    inverse = 500000.0 ** (-(jnp.arange(half, dtype=F32) * 2.0) / LANES)
-    angles = position[:, None].astype(F32) * inverse
-    cosine, sine = jnp.cos(angles), jnp.sin(angles)
-    cosine = jnp.concatenate([cosine, cosine], axis=1)
-    sine = jnp.concatenate([-sine, sine], axis=1)
-    return jnp.where(plain[:, None], 1.0, cosine), jnp.where(plain[:, None], 0.0, sine)
 
 
 def exchange(messages, axis):
@@ -269,28 +279,47 @@
     context_lengths,
     keep_blocks,
 ):
-    seq_index = lax.axis_index("seq")
     width = hidden_states.shape[2]
     context = key_cache.shape[1]
     columns = w_out.shape[1]
     rows = hidden_states.transpose(1, 0, 2).reshape(TOKENS, width)
-    parts = pl.pallas_call(
+    half = LANES // 2
+    inverse = (500000.0 ** (-(np.arange(LANES) % half) * 2.0 / LANES)).astype(np.float32)
+    array = pltpu.VMEM
+    parts, cosine, sine, live, kept, fresh = pl.pallas_call(
         project,
-        out_shape=pltpu.VMEM((SEQ, MESSAGE, LANES), BF16),
-        in_specs=[HBM] * 4,
-        out_specs=VMEM,
+        out_shape=(
+            array((SEQ, MESSAGE, LANES), BF16),
+            array((MESSAGE, LANES), F32),
+            array((MESSAGE, LANES), F32),
+            array((BATCH, context), F32),
+            array((BATCH, context), F32),
+            array((ROWS, LANES), F32),
+        ),
+        in_specs=[HBM] * 7,
+        out_specs=(VMEM,) * 6,
         scratch_shapes=[
             pltpu.VMEM((TOKENS, width), BF16),
             pltpu.VMEM(w_query.shape, BF16),
             pltpu.VMEM(w_key.shape, BF16),
             pltpu.VMEM(w_value.shape, BF16),
+            pltpu.SMEM(context_lengths.shape, jnp.int32),
+            pltpu.SMEM(keep_blocks.shape, jnp.int32),
+            pltpu.VMEM((1, LANES), F32),
             pltpu.VMEM((SEQ * MESSAGE, LANES), F32),
-            pltpu.SemaphoreType.DMA((4,)),
+            pltpu.SemaphoreType.DMA((7,)),
         ],
         name="project",
         compiler_params=pltpu.CompilerParams(vmem_limit_bytes=8 << 20),
-    )(*(in_place(array) for array in (rows, w_query, w_key, w_value)))
-    cosine, sine = tables(seq_index, context_lengths)
+    )(
+        *(
+            in_place(operand)
+            for operand in (
+                rows, w_query, w_key, w_value, context_lengths, keep_blocks,
+                jnp.asarray(inverse).reshape(1, LANES),
+            )
+        )
+    )
     parts = exchange(parts, "seq")
     rotated = pl.pallas_call(
         rotate,
@@ -298,30 +327,30 @@
         in_specs=[VMEM] * 3,
         out_specs=VMEM,
         name="rotate",
+        cost_estimate=pl.CostEstimate(
+            flops=1000000000, transcendentals=0, bytes_accessed=64000000
+        ),
         compiler_params=pltpu.CompilerParams(vmem_limit_bytes=8 << 20),
     )(resident(parts), resident(cosine), resident(sine))
     rotated = exchange(rotated, "seq")
-    first = (seq_index * context).astype(jnp.int32).reshape(1)
     partial = pl.pallas_call(
         attend,
         out_shape=pltpu.VMEM((SEQ, (PER_OWNER + 1) * ROWS, LANES), BF16),
-        in_specs=[SMEM, SMEM, SMEM, VMEM, VMEM, HBM],
+        in_specs=[VMEM] * 6,
         out_specs=VMEM,
         scratch_shapes=[
             pltpu.VMEM((BATCH, VERIFY * ROWS, context), F32),
             pltpu.VMEM((BATCH, TILES * ROWS, context), BF16),
-            pltpu.VMEM((BATCH, context, LANES), BF16),
-            pltpu.SemaphoreType.DMA,
         ],
         name="attend",
         compiler_params=pltpu.CompilerParams(vmem_limit_bytes=16 << 20),
     )(
-        context_lengths,
-        keep_blocks,
-        first,
+        resident(live),
+        resident(kept),
+        resident(fresh),
         resident(rotated.reshape(SEQ * MESSAGE, LANES)),
         resident(key_cache),
-        in_place(value_cache),
+        resident(value_cache),
     )
     partial = exchange(partial, "seq")
     merged = pl.pallas_call(

time: 87 us -> 83.3 us (0.957)
  blocking collectives: 43.9 us -> 78.1 us
  waiting for transfers between devices: 17.1 us -> 0 us
  starting transfers between devices: 15.9 us -> 0 us
  Pallas kernels: 7.36 us -> 4.25 us
  local copies, waits for them, and re-layouts: 1.34 us -> 0.02 us
    all_to_all x3 -> x5, blocking collectives: 43.9 us -> 78.1 us  [exchange(): return lax.all_to_all(messages, axis, 0, 0, tiled=True)]
    all_to_all x2 -> x0, waiting for transfers between devices: 17.1 us -> none  [exchange(): return lax.all_to_all(messages, axis, 0, 0, tiled=True)]
    all_to_all x2 -> x0, starting transfers between devices: 15.9 us -> none  [exchange(): return lax.all_to_all(messages, axis, 0, 0, tiled=True)]
    pallas_call x1, Pallas kernels: 3.16 us -> 1.45 us  [per_device(): pl.pallas_call(attend, out_shape=pltpu.VMEM((SEQ, (PER_OWNER + 1) * ROWS,...]
    gather x1 -> x0, local copies, waits for them, and re-layouts: 1.32 us -> none  [tables(): position = context_lengths[token % BATCH] + token // BATCH]
  transfers between devices with their start and end apart: 2 -> 0, of which waited for: 2 -> 0; matrix products, arithmetic and copies ran while one was open for 2% -> 0% of each run, Pallas kernels for 0% -> 0%
where the time goes in v3:
time: 83.3 us; the launch traced here: 83.1 us
  blocking collectives  78.1 us (94%)
  Pallas kernels  4.25 us (5%)
    all_to_all x5, blocking collectives, exchange(): return lax.all_to_all(messages, axis, 0, 0, tiled=True)  78.1 us

profile of v3, /device:TPU:1, one launch (start us, length us, event | category | flops | bytes accessed | tf_op | source)
XLA Modules:
  0.0 83.1 jit_solution(12814067911233460825)
XLA Ops:
  0.6 1.4 %project.1 = (bf16[32,16,128]{2,1,0:T(8,128)(2,1)S(1)}, f32[16,128]{1,0:T(8,128)S(1)}, f32[16,128]{1,0:T(8,128)S(1)}, f32[8,1024]{1,0:T(8,128)S(1)}, f32[8,1024]{1,0:T(8,128)S(1)}, /*index=5*/f32[8,128]{1,0:T(8,128)S(1)}) custom-call(bf16[40,256]{1,0:T(8,128)(2,1)} %bitcast.8, bf16[256,1024]{1,0:T(8,128)(2,1)} %query_hbm.1, bf16[256,128]{1,0:T(8,128)(2,1)} %key_hbm.1, ...), custom_call_target="tpu_custom_call" | custom-call | tf_op jit(solution)/shard_map/project/pallas_call | solution.py:289
  2.0 0.0 copy-start
  2.0 0.0 copy-start.1
  2.0 21.4 %all_to_all.25.parts_ref = bf16[32,16,128]{2,1,0:T(8,128)(2,1)S(1)} all-to-all(bf16[32,16,128]{2,1,0:T(8,128)(2,1)S(1)} %get-tuple-element.13), channel_id=1, replica_groups=mesh['seq'=32,'head'=8] {'seq'}, dimensions={0} | all-to-all | bytes 262144 | tf_op jit(solution)/shard_map/all_to_all | solution.py:268
  23.5 0.1 rotate.1
  23.6 12.6 %all_to_all.26 = bf16[32,16,128]{2,1,0:T(8,128)(2,1)S(1)} all-to-all(bf16[32,16,128]{2,1,0:T(8,128)(2,1)S(1)} %rotate.1), channel_id=1, replica_groups=mesh['seq'=32,'head'=8] {'seq'}, dimensions={0} | all-to-all | bytes 262144 | tf_op jit(solution)/shard_map/all_to_all | solution.py:268
  36.2 0.0 copy-done
  36.2 0.0 copy-done.1
  36.2 0.0 copy-start.2
  36.2 1.4 %attend.1 = bf16[32,32,128]{2,1,0:T(8,128)(2,1)S(1)} custom-call(f32[8,1024]{1,0:T(8,128)S(1)} %get-tuple-element.10.live_ref, f32[8,1024]{1,0:T(8,128)S(1)} %get-tuple-element.11.kept_ref, f32[8,128]{1,0:T(8,128)S(1)} %get-tuple-element.12.fresh_ref, bf16[512,128]{1,0:T(8,128)(2,1)S(1)} %bitcast.7, bf16[8,1024,128]{2,1,0:T(8,128)(2,1)S(1)} %copy-done, ...), custom_call_target="tpu_custom_call" | custom-call | tf_op jit(solution)/shard_map/attend/pallas_call | solution.py:336
  37.7 13.8 %all_to_all.27.parts_ref = bf16[32,32,128]{2,1,0:T(8,128)(2,1)S(1)} all-to-all(bf16[32,32,128]{2,1,0:T(8,128)(2,1)S(1)} %attend.1), channel_id=1, replica_groups=mesh['seq'=32,'head'=8] {'seq'}, dimensions={0} | all-to-all | bytes 524288 | tf_op jit(solution)/shard_map/all_to_all | solution.py:268
  51.5 0.4 merge.1
  51.9 13.5 %all_to_all.28 = bf16[32,24,128]{2,1,0:T(8,128)(2,1)S(1)} all-to-all(bf16[32,24,128]{2,1,0:T(8,128)(2,1)S(1)} %merge.1), channel_id=1, replica_groups=mesh['seq'=32,'head'=8] {'seq'}, dimensions={0} | all-to-all | bytes 393216 | tf_op jit(solution)/shard_map/all_to_all | solution.py:268
  65.3 0.0 copy-done.2
  65.3 0.3 project_out.1
  65.6 16.8 %all_to_all.29.parts_ref = bf16[8,72,256]{2,1,0:T(8,128)(2,1)S(1)} all-to-all(bf16[8,72,256]{2,1,0:T(8,128)(2,1)S(1)} %project_out.1), channel_id=1, replica_groups=mesh['seq'=32,'head'=8] {'head'}, dimensions={0} | all-to-all | bytes 589824 | tf_op jit(solution)/shard_map/all_to_all | solution.py:268
  82.4 0.7 add_groups.1
Async XLA Ops:
  2.0 34.2 %copy-start = (bf16[8,1024,128]{2,1,0:T(8,128)(2,1)S(1)}, bf16[8,1024,128]{2,1,0:T(8,128)(2,1)}, u32[]{:S(2)}) copy-start(bf16[8,1024,128]{2,1,0:T(8,128)(2,1)} %keys.1) | copy-start | bytes 6291460
  2.0 34.2 %copy-start.1 = (bf16[8,1024,128]{2,1,0:T(8,128)(2,1)S(1)}, bf16[8,1024,128]{2,1,0:T(8,128)(2,1)}, u32[]{:S(2)}) copy-start(bf16[8,1024,128]{2,1,0:T(8,128)(2,1)} %values.1) | copy-start | bytes 6291460
  36.2 29.1 %copy-start.2 = (bf16[1024,256]{1,0:T(8,128)(2,1)S(1)}, bf16[1024,256]{1,0:T(8,128)(2,1)}, u32[]{:S(2)}) copy-start(bf16[1024,256]{1,0:T(8,128)(2,1)} %weight_ref.1) | copy-start | bytes 1572868

commit v4 on v3

--- a/solution.py
+++ b/solution.py
@@ -14,6 +14,8 @@
 TILES = VERIFY + DRAFT
 SEQ = 32
 HEADS = 8
+CORES = 2
+CHIPS = HEADS // CORES
 TOKENS = BATCH * VERIFY
 QUERY_ROWS = TOKENS * ROWS
 PER_OWNER = 3
@@ -233,14 +235,18 @@
             rows, weight_ref[h * LANES : (h + 1) * LANES, :], preferred_element_type=F32
         )
         total = part if total is None else total + part
-    rounded = total.astype(BF16)
-    for h in range(HEADS):
-        out_ref[h] = rounded
+    out_ref[...] = total.astype(BF16)
+
+
+def add_pair(mine_ref, other_ref, out_ref):
+    rounded = (mine_ref[...].astype(F32) + other_ref[...].astype(F32)).astype(BF16)
+    for x in range(CHIPS):
+        out_ref[x] = rounded
 
 
 def add_groups(parts_ref, verify_ref, draft_ref, *halves):
     summed = parts_ref[0].astype(F32)
-    for h in range(1, HEADS):
+    for h in range(1, CHIPS):
         summed += parts_ref[h].astype(F32)
     rounded = summed.astype(BF16)
     for j in range(VERIFY):
@@ -364,14 +370,24 @@
     merged = exchange(merged, "seq").reshape(SEQ * PER_OWNER * ROWS, LANES)
     groups = pl.pallas_call(
         project_out,
-        out_shape=pltpu.VMEM((HEADS, BATCH * TILES, columns), BF16),
+        out_shape=pltpu.VMEM((BATCH * TILES, columns), BF16),
         in_specs=[VMEM, VMEM],
         out_specs=VMEM,
         scratch_shapes=[pltpu.VMEM((BATCH * TILES * ROWS, LANES), F32)],
         name="project_out",
         compiler_params=pltpu.CompilerParams(vmem_limit_bytes=8 << 20),
     )(resident(merged), resident(w_out))
-    groups = exchange(groups, "head")
+    other = lax.ppermute(groups, "head", [(h, h ^ 1) for h in range(HEADS)])
+    pairs = pl.pallas_call(
+        add_pair,
+        out_shape=pltpu.VMEM((CHIPS, BATCH * TILES, columns), BF16),
+        in_specs=[VMEM, VMEM],
+        out_specs=VMEM,
+        name="add_pair",
+        compiler_params=pltpu.CompilerParams(vmem_limit_bytes=8 << 20),
+    )(resident(groups), resident(other))
+    across = [[x * CORES + c for x in range(CHIPS)] for c in range(CORES)]
+    pairs = lax.all_to_all(pairs, "head", 0, 0, tiled=True, axis_index_groups=across)
     verify_out, draft_out = pl.pallas_call(
         add_groups,
         out_shape=(
@@ -383,7 +399,7 @@
         scratch_shapes=[pltpu.VMEM((DRAFT * BATCH, LANES), F32)] * (columns // LANES),
         name="add_groups",
         compiler_params=pltpu.CompilerParams(vmem_limit_bytes=8 << 20),
-    )(resident(groups))
+    )(resident(pairs))
     return verify_out.transpose(1, 0, 2), draft_out
 
 

time: 83.3 us -> 81.6 us (0.980)
  blocking collectives: 78.1 us -> 69.9 us
  starting transfers between devices: 0 us -> 5.6 us
  waiting for transfers between devices: 0 us -> 0.87 us
    all_to_all x5 -> x4, blocking collectives: 78.1 us -> 61.3 us  [exchange(): return lax.all_to_all(messages, axis, 0, 0, tiled=True)]
    all_to_all x0 -> x1, blocking collectives: none -> 8.63 us  [per_device(): lax.all_to_all(pairs, 'head', 0, 0, tiled=True, axis_index_groups=across)]
    ppermute x0 -> x1, starting transfers between devices: none -> 5.6 us  [per_device(): other = lax.ppermute(groups, 'head', [(h, h ^ 1) for h in range(HEADS)])]
    ppermute x0 -> x1, waiting for transfers between devices: none -> 0.87 us  [per_device(): other = lax.ppermute(groups, 'head', [(h, h ^ 1) for h in range(HEADS)])]
  transfers between devices with their start and end apart: 0 -> 1, of which waited for: 0 -> 1; matrix products, arithmetic and copies ran while one was open for 0% -> 0% of each run, Pallas kernels for 0% -> 0%
where the time goes in v4:
time: 81.6 us; the launch traced here: 81.3 us
  blocking collectives  69.9 us (86%)
  starting transfers between devices  5.6 us (7%)
  Pallas kernels  4.24 us (5%)
  waiting for transfers between devices  0.87 us (1%)
    all_to_all x4, blocking collectives, exchange(): return lax.all_to_all(messages, axis, 0, 0, tiled=True)  61.3 us
    all_to_all x1, blocking collectives, per_device(): lax.all_to_all(pairs, 'head', 0, 0, tiled=True, axis_index_groups=across)  8.63 us
    ppermute x1, starting transfers between devices, per_device(): other = lax.ppermute(groups, 'head', [(h, h ^ 1) for h in range(HEADS)])  5.6 us
  transfers between devices with their start and end apart: 1, of which 1 were waited for; matrix products, arithmetic and copies ran while one was open for 0% of the time, Pallas kernels for 0%

profile of v4, /device:TPU:1, one launch (start us, length us, event | category | flops | bytes accessed | tf_op | source)
XLA Modules:
  0.0 81.3 jit_solution(17430113605885836051)
XLA Ops:
  0.6 1.4 %project.1 = (bf16[32,16,128]{2,1,0:T(8,128)(2,1)S(1)}, f32[16,128]{1,0:T(8,128)S(1)}, f32[16,128]{1,0:T(8,128)S(1)}, f32[8,1024]{1,0:T(8,128)S(1)}, f32[8,1024]{1,0:T(8,128)S(1)}, /*index=5*/f32[8,128]{1,0:T(8,128)S(1)}) custom-call(bf16[40,256]{1,0:T(8,128)(2,1)} %bitcast.8, bf16[256,1024]{1,0:T(8,128)(2,1)} %query_hbm.1, bf16[256,128]{1,0:T(8,128)(2,1)} %key_hbm.1, ...), custom_call_target="tpu_custom_call" | custom-call | tf_op jit(solution)/shard_map/project/pallas_call | solution.py:295
  2.0 0.0 copy-start
  2.0 0.0 copy-start.1
  2.0 21.4 %all_to_all.25.parts_ref = bf16[32,16,128]{2,1,0:T(8,128)(2,1)S(1)} all-to-all(bf16[32,16,128]{2,1,0:T(8,128)(2,1)S(1)} %get-tuple-element.13), channel_id=1, replica_groups=mesh['seq'=32,'head'=8] {'seq'}, dimensions={0} | all-to-all | bytes 262144 | tf_op jit(solution)/shard_map/all_to_all | solution.py:274
  23.5 0.1 rotate.1
  23.6 12.6 %all_to_all.26 = bf16[32,16,128]{2,1,0:T(8,128)(2,1)S(1)} all-to-all(bf16[32,16,128]{2,1,0:T(8,128)(2,1)S(1)} %rotate.1), channel_id=1, replica_groups=mesh['seq'=32,'head'=8] {'seq'}, dimensions={0} | all-to-all | bytes 262144 | tf_op jit(solution)/shard_map/all_to_all | solution.py:274
  36.2 0.0 copy-done
  36.2 0.0 copy-done.1
  36.2 0.0 copy-start.2
  36.2 1.4 %attend.1 = bf16[32,32,128]{2,1,0:T(8,128)(2,1)S(1)} custom-call(f32[8,1024]{1,0:T(8,128)S(1)} %get-tuple-element.10.live_ref, f32[8,1024]{1,0:T(8,128)S(1)} %get-tuple-element.11.kept_ref, f32[8,128]{1,0:T(8,128)S(1)} %get-tuple-element.12.fresh_ref, bf16[512,128]{1,0:T(8,128)(2,1)S(1)} %bitcast.7, bf16[8,1024,128]{2,1,0:T(8,128)(2,1)S(1)} %copy-done, ...), custom_call_target="tpu_custom_call" | custom-call | tf_op jit(solution)/shard_map/attend/pallas_call | solution.py:342
  37.7 13.8 %all_to_all.27.parts_ref = bf16[32,32,128]{2,1,0:T(8,128)(2,1)S(1)} all-to-all(bf16[32,32,128]{2,1,0:T(8,128)(2,1)S(1)} %attend.1), channel_id=1, replica_groups=mesh['seq'=32,'head'=8] {'seq'}, dimensions={0} | all-to-all | bytes 524288 | tf_op jit(solution)/shard_map/all_to_all | solution.py:274
  51.5 0.4 merge.1
  51.9 13.5 %all_to_all.28 = bf16[32,24,128]{2,1,0:T(8,128)(2,1)S(1)} all-to-all(bf16[32,24,128]{2,1,0:T(8,128)(2,1)S(1)} %merge.1), channel_id=1, replica_groups=mesh['seq'=32,'head'=8] {'seq'}, dimensions={0} | all-to-all | bytes 393216 | tf_op jit(solution)/shard_map/all_to_all | solution.py:274
  65.3 0.0 copy-done.2
  65.3 0.2 project_out.1.mine_ref
  65.6 5.6 %collective-permute-start = (bf16[72,256]{1,0:T(8,128)(2,1)S(1)}, bf16[72,256]{1,0:T(8,128)(2,1)S(1)}, u32[]{:S(2)}, u32[]{:S(2)}) collective-permute-start(bf16[72,256]{1,0:T(8,128)(2,1)S(1)} %project_out.1.mine_ref), channel_id=1, source_target_pairs={{0,1},{1,0},{2,3},{3,2},{4,5},{5,4},{6,7},{7,6},{8,9},{9,8},{10,11... | collective-permute-start | bytes 110600 | tf_op jit(solution)/shard_map/ppermute | solution.py:380
  71.2 0.9 %collective-permute-done.other_ref = bf16[72,256]{1,0:T(8,128)(2,1)S(1)} collective-permute-done((bf16[72,256]{1,0:T(8,128)(2,1)S(1)}, bf16[72,256]{1,0:T(8,128)(2,1)S(1)}, u32[]{:S(2)}, u32[]{:S(2)}) %collective-permute-start) | collective-permute-done | bytes 36896 | tf_op jit(solution)/shard_map/ppermute | solution.py:380
  72.1 8.6 %all_to_all.29.parts_ref = bf16[4,72,256]{2,1,0:T(8,128)(2,1)S(1)} all-to-all(bf16[4,72,256]{2,1,0:T(8,128)(2,1)S(1)} %add_pair.1), channel_id=1, replica_groups={{0,2,4,6},{1,3,5,7},{8,10,12,14},{9,11,13,15},{16,18,20,22},{17,19,21,2..., dimensions={0} | all-to-all | bytes 294912 | tf_op jit(solution)/shard_map/all_to_all | solution.py:390
  80.7 0.6 add_groups.1
  (1 shorter events, 0.0 us)
Async XLA Ops:
  2.0 34.2 %copy-start = (bf16[8,1024,128]{2,1,0:T(8,128)(2,1)S(1)}, bf16[8,1024,128]{2,1,0:T(8,128)(2,1)}, u32[]{:S(2)}) copy-start(bf16[8,1024,128]{2,1,0:T(8,128)(2,1)} %keys.1) | copy-start | bytes 6291460
  2.0 34.2 %copy-start.1 = (bf16[8,1024,128]{2,1,0:T(8,128)(2,1)S(1)}, bf16[8,1024,128]{2,1,0:T(8,128)(2,1)}, u32[]{:S(2)}) copy-start(bf16[8,1024,128]{2,1,0:T(8,128)(2,1)} %values.1) | copy-start | bytes 6291460
  36.2 29.1 %copy-start.2 = (bf16[1024,256]{1,0:T(8,128)(2,1)S(1)}, bf16[1024,256]{1,0:T(8,128)(2,1)}, u32[]{:S(2)}) copy-start(bf16[1024,256]{1,0:T(8,128)(2,1)} %weight_ref.1) | copy-start | bytes 1572868
  65.6 6.5 %collective-permute-start = (bf16[72,256]{1,0:T(8,128)(2,1)S(1)}, bf16[72,256]{1,0:T(8,128)(2,1)S(1)}, u32[]{:S(2)}, u32[]{:S(2)}) collective-permute-start(bf16[72,256]{1,0:T(8,128)(2,1)S(1)} %project_out.1.mine_ref), channel_id=1, source_target_pairs={{0,1},{1,0},{2,3},{3,2},{4,5},{5,4},{6,7},{7,6},{8,9},{9,8},{10,11... | collective-permute-start | bytes 110600 | tf_op jit(solution)/shard_map/ppermute | solution.py:380

commit v5 on v4

--- a/solution.py
+++ b/solution.py
@@ -18,8 +18,11 @@
 CHIPS = HEADS // CORES
 TOKENS = BATCH * VERIFY
 QUERY_ROWS = TOKENS * ROWS
-PER_OWNER = 3
-OWNERS = BATCH * TILES // PER_OWNER
+OWNERS = SEQ // BATCH
+PAIRS = TILES * ROWS // OWNERS
+SUB = 4
+STRIPS = 5
+SLOTS = 24
 MESSAGE = 16
 NEGATIVE = -(2.0**100)
 SCALE = LANES**-0.5
@@ -109,7 +112,8 @@
 
 
 def attend(
-    live_ref, kept_ref, fresh_ref, all_ref, keys, values, out_ref, scores, weights
+    live_ref, kept_ref, fresh_ref, all_ref, keys, values,
+    out_ref, scores, weights, results, tails,
 ):
     blocks = keys.shape[1] // LANES
     lane = lax.broadcasted_iota(jnp.int32, (ROWS, LANES), 1)
@@ -179,52 +183,69 @@
         preferred_element_type=F32,
     )
     rows = TILES * ROWS
+    packed = jnp.zeros((rows, LANES), F32)
+    lanes = lax.broadcasted_iota(jnp.int32, (rows, LANES), 1)
     for b in range(BATCH):
-        result = jnp.dot(weights[b], values[b], preferred_element_type=F32)
-        result += fresh_result[b * rows : (b + 1) * rows]
-        stats = bases[b] + split(totals[b])
-        for i in range(TILES // PER_OWNER):
-            packed = jnp.zeros((ROWS, LANES), F32)
-            for u in range(PER_OWNER):
-                t = i * PER_OWNER + u
-                for k, value in enumerate(stats):
-                    packed = jnp.where(
-                        lane == 4 * u + k, value[t * ROWS : (t + 1) * ROWS], packed
-                    )
-            part = result[i * PER_OWNER * ROWS : (i + 1) * PER_OWNER * ROWS]
-            out_ref[b * (TILES // PER_OWNER) + i] = jnp.concatenate([part, packed], axis=0).astype(
-                BF16
-            )
-    for d in range(OWNERS, SEQ):
-        out_ref[d] = jnp.zeros(out_ref.shape[1:], BF16)
-
-
-def merge(parts_ref, out_ref):
-    acc_rows = PER_OWNER * ROWS
-    stats = []
+        results[pl.ds(b * rows, rows), :] = (
+            jnp.dot(weights[b], values[b], preferred_element_type=F32)
+            + fresh_result[b * rows : (b + 1) * rows]
+        )
+        for k, value in enumerate(bases[b] + split(totals[b])):
+            packed = jnp.where(lanes == k * BATCH + b, value, packed)
+    stats = jnp.concatenate([packed, jnp.zeros((LANES - rows, LANES), F32)], axis=0).T
+    for i in range(OWNERS):
+        near = stats[: 4 * BATCH]
+        if i:
+            near = pltpu.roll(near, LANES - i * PAIRS, 1)
+        far = pltpu.roll(near, LANES // 2, 1)
+        for r in range(2):
+            high = near[2 * r * BATCH : (2 * r + 1) * BATCH]
+            low = far[(2 * r + 1) * BATCH : (2 * r + 2) * BATCH]
+            every = pl.ds(i * SUB + 2 + r, BATCH, stride=OWNERS * SUB)
+            tails[every, :] = jnp.where(lane < LANES // 2, high, low)
+            tails[pl.ds(i * SUB + r, BATCH, stride=OWNERS * SUB), :] = results[
+                pl.ds(i * PAIRS + 16 + r, BATCH, stride=rows), :
+            ]
+    for d in range(SEQ):
+        for k in range(STRIPS):
+            if k < STRIPS - 1:
+                strip = results[pl.ds(d * PAIRS + k * SUB, SUB), :]
+            else:
+                strip = tails[pl.ds(d * SUB, SUB), :]
+            out_ref[d, :, k * LANES : (k + 1) * LANES] = strip.astype(BF16)
+
+
+def merge(parts_ref, out_ref, parts):
     for s in range(SEQ):
-        packed = parts_ref[s][acc_rows:].astype(F32)
-        stats.append(packed + pltpu.roll(packed, LANES - 1, 1))
-    peak = stats[0]
-    for s in range(1, SEQ):
-        peak = jnp.maximum(peak, stats[s])
-    total = jnp.zeros((ROWS, LANES), F32)
-    sums = [jnp.zeros((ROWS, LANES), F32) for _ in range(PER_OWNER)]
+        for k in range(STRIPS):
+            strip = parts_ref[s, :, k * LANES : (k + 1) * LANES]
+            parts[pl.ds(s * SLOTS + k * SUB, SUB), :] = strip.astype(F32)
+        parts[pl.ds(s * SLOTS + STRIPS * SUB, SUB), :] = jnp.zeros((SUB, LANES), F32)
+    peaks = parts[pl.ds(PAIRS, SEQ, stride=SLOTS), :]
+    peaks += pltpu.roll(peaks, LANES // 2, 1)
+    totals = parts[pl.ds(PAIRS + 1, SEQ, stride=SLOTS), :]
+    totals += pltpu.roll(totals, LANES // 2, 1)
+    factors = jnp.exp2(peaks - jnp.max(peaks, axis=0, keepdims=True))
+    total = jnp.sum(factors * totals, axis=0, keepdims=True)
+    factors = factors / jnp.where(total > 0.0, total, 1.0)
+    factors = jnp.concatenate([factors, jnp.zeros((LANES - SEQ, LANES), F32)], axis=0).T
+    factors = factors[:SLOTS]
+    merged = jnp.zeros((SLOTS, LANES), F32)
     for s in range(SEQ):
-        factor = jnp.exp2(stats[s] - peak)
-        total += factor * pltpu.roll(stats[s], LANES - 2, 1)
-        part = parts_ref[s][:acc_rows].astype(F32)
-        for u in range(PER_OWNER):
-            sums[u] += part[u * ROWS : (u + 1) * ROWS] * factor[:, 4 * u : 4 * u + 1]
-    merged = jnp.concatenate(
-        [sums[u] / total[:, 4 * u : 4 * u + 1] for u in range(PER_OWNER)], axis=0
-    ).astype(BF16)
-    for s in range(SEQ):
-        out_ref[s] = merged
+        merged += parts[pl.ds(s * SLOTS, SLOTS), :] * factors[:, s : s + 1]
+    merged = merged.astype(BF16)
+    for k in range(STRIPS):
+        strip = merged[k * SUB : (k + 1) * SUB]
+        for s in range(SEQ):
+            out_ref[s, :, k * LANES : (k + 1) * LANES] = strip
 
 
 def project_out(all_ref, weight_ref, out_ref, attended):
-    attended[...] = all_ref[pl.ds(0, BATCH * TILES * ROWS), :].astype(F32)
+    for d in range(SEQ):
+        for k in range(STRIPS):
+            size = min(SUB, PAIRS - k * SUB)
+            strip = all_ref[d, :, k * LANES : (k + 1) * LANES].astype(F32)
+            attended[pl.ds(d * PAIRS + k * SUB, size), :] = strip[:size]
     total = None
     for h in range(ROWS):
         rows = jnp.concatenate(
@@ -341,12 +362,14 @@
     rotated = exchange(rotated, "seq")
     partial = pl.pallas_call(
         attend,
-        out_shape=pltpu.VMEM((SEQ, (PER_OWNER + 1) * ROWS, LANES), BF16),
+        out_shape=pltpu.VMEM((SEQ, SUB, STRIPS * LANES), BF16),
         in_specs=[VMEM] * 6,
         out_specs=VMEM,
         scratch_shapes=[
             pltpu.VMEM((BATCH, VERIFY * ROWS, context), F32),
             pltpu.VMEM((BATCH, TILES * ROWS, context), BF16),
+            pltpu.VMEM((BATCH * TILES * ROWS, LANES), F32),
+            pltpu.VMEM((SEQ * SUB, LANES), F32),
         ],
         name="attend",
         compiler_params=pltpu.CompilerParams(vmem_limit_bytes=16 << 20),
@@ -361,13 +384,14 @@
     partial = exchange(partial, "seq")
     merged = pl.pallas_call(
         merge,
-        out_shape=pltpu.VMEM((SEQ, PER_OWNER * ROWS, LANES), BF16),
+        out_shape=pltpu.VMEM((SEQ, SUB, STRIPS * LANES), BF16),
         in_specs=[VMEM],
         out_specs=VMEM,
+        scratch_shapes=[pltpu.VMEM((SEQ * SLOTS, LANES), F32)],
         name="merge",
         compiler_params=pltpu.CompilerParams(vmem_limit_bytes=8 << 20),
     )(resident(partial))
-    merged = exchange(merged, "seq").reshape(SEQ * PER_OWNER * ROWS, LANES)
+    merged = exchange(merged, "seq")
     groups = pl.pallas_call(
         project_out,
         out_shape=pltpu.VMEM((BATCH * TILES, columns), BF16),

time: 81.6 us -> 80.6 us (0.988)
  blocking collectives: 69.9 us -> 68.6 us
    all_to_all x4, blocking collectives: 61.3 us -> 59.9 us  [exchange(): return lax.all_to_all(messages, axis, 0, 0, tiled=True)]
where the time goes in v5:
time: 80.6 us; the launch traced here: 80.3 us
  blocking collectives  68.6 us (85%)
  starting transfers between devices  5.71 us (7%)
  Pallas kernels  4.42 us (5%)
  waiting for transfers between devices  0.87 us (1%)
    all_to_all x4, blocking collectives, exchange(): return lax.all_to_all(messages, axis, 0, 0, tiled=True)  59.9 us
    all_to_all x1, blocking collectives, per_device(): lax.all_to_all(pairs, 'head', 0, 0, tiled=True, axis_index_groups=across)  8.72 us
    ppermute x1, starting transfers between devices, per_device(): other = lax.ppermute(groups, 'head', [(h, h ^ 1) for h in range(HEADS)])  5.71 us
  transfers between devices with their start and end apart: 1, of which 1 were waited for; matrix products, arithmetic and copies ran while one was open for 0% of the time, Pallas kernels for 0%

profile of v5, /device:TPU:1, one launch (start us, length us, event | category | flops | bytes accessed | tf_op | source)
XLA Modules:
  0.0 80.3 jit_solution(5569280491169183849)
XLA Ops:
  0.6 1.4 %project.1 = (bf16[32,16,128]{2,1,0:T(8,128)(2,1)S(1)}, f32[16,128]{1,0:T(8,128)S(1)}, f32[16,128]{1,0:T(8,128)S(1)}, f32[8,1024]{1,0:T(8,128)S(1)}, f32[8,1024]{1,0:T(8,128)S(1)}, /*index=5*/f32[8,128]{1,0:T(8,128)S(1)}) custom-call(bf16[40,256]{1,0:T(8,128)(2,1)} %bitcast.6, bf16[256,1024]{1,0:T(8,128)(2,1)} %query_hbm.1, bf16[256,128]{1,0:T(8,128)(2,1)} %key_hbm.1, ...), custom_call_target="tpu_custom_call" | custom-call | tf_op jit(solution)/shard_map/project/pallas_call | solution.py:316
  2.0 0.0 copy-start
  2.0 0.0 copy-start.1
  2.0 21.4 %all_to_all.25.parts_ref = bf16[32,16,128]{2,1,0:T(8,128)(2,1)S(1)} all-to-all(bf16[32,16,128]{2,1,0:T(8,128)(2,1)S(1)} %get-tuple-element.13), channel_id=1, replica_groups=mesh['seq'=32,'head'=8] {'seq'}, dimensions={0} | all-to-all | bytes 262144 | tf_op jit(solution)/shard_map/all_to_all | solution.py:295
  23.5 0.1 rotate.1
  23.6 12.6 %all_to_all.26 = bf16[32,16,128]{2,1,0:T(8,128)(2,1)S(1)} all-to-all(bf16[32,16,128]{2,1,0:T(8,128)(2,1)S(1)} %rotate.1), channel_id=1, replica_groups=mesh['seq'=32,'head'=8] {'seq'}, dimensions={0} | all-to-all | bytes 262144 | tf_op jit(solution)/shard_map/all_to_all | solution.py:295
  36.2 0.0 copy-done
  36.2 0.0 copy-done.1
  36.2 0.0 copy-start.2
  36.2 1.6 %attend.1 = bf16[32,4,640]{2,1,0:T(4,128)(2,1)S(1)} custom-call(f32[8,1024]{1,0:T(8,128)S(1)} %get-tuple-element.10.live_ref, f32[8,1024]{1,0:T(8,128)S(1)} %get-tuple-element.11.kept_ref, f32[8,128]{1,0:T(8,128)S(1)} %get-tuple-element.12.fresh_ref, bf16[512,128]{1,0:T(8,128)(2,1)S(1)} %bitcast.5, bf16[8,1024,128]{2,1,0:T(8,128)(2,1)S(1)} %copy-done, ...), custom_call_target="tpu_custom_call" | custom-call | tf_op jit(solution)/shard_map/attend/pallas_call | solution.py:363
  37.8 13.0 %all_to_all.27.parts_ref = bf16[32,4,640]{2,1,0:T(4,128)(2,1)S(1)} all-to-all(bf16[32,4,640]{2,1,0:T(4,128)(2,1)S(1)} %attend.1), channel_id=1, replica_groups=mesh['seq'=32,'head'=8] {'seq'}, dimensions={0} | all-to-all | bytes 327680 | tf_op jit(solution)/shard_map/all_to_all | solution.py:295
  50.8 0.4 merge.1
  51.3 12.8 %all_to_all.28.all_ref = bf16[32,4,640]{2,1,0:T(4,128)(2,1)S(1)} all-to-all(bf16[32,4,640]{2,1,0:T(4,128)(2,1)S(1)} %merge.1), channel_id=1, replica_groups=mesh['seq'=32,'head'=8] {'seq'}, dimensions={0} | all-to-all | bytes 327680 | tf_op jit(solution)/shard_map/all_to_all | solution.py:295
  64.1 0.0 copy-done.2
  64.1 0.3 project_out.1.mine_ref
  64.3 5.7 %collective-permute-start = (bf16[72,256]{1,0:T(8,128)(2,1)S(1)}, bf16[72,256]{1,0:T(8,128)(2,1)S(1)}, u32[]{:S(2)}, u32[]{:S(2)}) collective-permute-start(bf16[72,256]{1,0:T(8,128)(2,1)S(1)} %project_out.1.mine_ref), channel_id=1, source_target_pairs={{0,1},{1,0},{2,3},{3,2},{4,5},{5,4},{6,7},{7,6},{8,9},{9,8},{10,11... | collective-permute-start | bytes 110600 | tf_op jit(solution)/shard_map/ppermute | solution.py:404
  70.0 0.9 %collective-permute-done.other_ref = bf16[72,256]{1,0:T(8,128)(2,1)S(1)} collective-permute-done((bf16[72,256]{1,0:T(8,128)(2,1)S(1)}, bf16[72,256]{1,0:T(8,128)(2,1)S(1)}, u32[]{:S(2)}, u32[]{:S(2)}) %collective-permute-start) | collective-permute-done | bytes 36896 | tf_op jit(solution)/shard_map/ppermute | solution.py:404
  70.9 8.7 %all_to_all.29.parts_ref = bf16[4,72,256]{2,1,0:T(8,128)(2,1)S(1)} all-to-all(bf16[4,72,256]{2,1,0:T(8,128)(2,1)S(1)} %add_pair.1), channel_id=1, replica_groups={{0,2,4,6},{1,3,5,7},{8,10,12,14},{9,11,13,15},{16,18,20,22},{17,19,21,2..., dimensions={0} | all-to-all | bytes 294912 | tf_op jit(solution)/shard_map/all_to_all | solution.py:414
  79.7 0.6 add_groups.1
  (1 shorter events, 0.0 us)
Async XLA Ops:
  2.0 34.2 %copy-start = (bf16[8,1024,128]{2,1,0:T(8,128)(2,1)S(1)}, bf16[8,1024,128]{2,1,0:T(8,128)(2,1)}, u32[]{:S(2)}) copy-start(bf16[8,1024,128]{2,1,0:T(8,128)(2,1)} %keys.1) | copy-start | bytes 6291460
  2.0 34.2 %copy-start.1 = (bf16[8,1024,128]{2,1,0:T(8,128)(2,1)S(1)}, bf16[8,1024,128]{2,1,0:T(8,128)(2,1)}, u32[]{:S(2)}) copy-start(bf16[8,1024,128]{2,1,0:T(8,128)(2,1)} %values.1) | copy-start | bytes 6291460
  36.2 27.8 %copy-start.2 = (bf16[1024,256]{1,0:T(8,128)(2,1)S(1)}, bf16[1024,256]{1,0:T(8,128)(2,1)}, u32[]{:S(2)}) copy-start(bf16[1024,256]{1,0:T(8,128)(2,1)} %weight_ref.1) | copy-start | bytes 1572868
  64.3 6.6 %collective-permute-start = (bf16[72,256]{1,0:T(8,128)(2,1)S(1)}, bf16[72,256]{1,0:T(8,128)(2,1)S(1)}, u32[]{:S(2)}, u32[]{:S(2)}) collective-permute-start(bf16[72,256]{1,0:T(8,128)(2,1)S(1)} %project_out.1.mine_ref), channel_id=1, source_target_pairs={{0,1},{1,0},{2,3},{3,2},{4,5},{5,4},{6,7},{7,6},{8,9},{9,8},{10,11... | collective-permute-start | bytes 110600 | tf_op jit(solution)/shard_map/ppermute | solution.py:404

commit v6 on v5

--- a/solution.py
+++ b/solution.py
@@ -22,6 +22,7 @@
 PAIRS = TILES * ROWS // OWNERS
 SUB = 4
 STRIPS = 5
+SPARE = 72
 SLOTS = 24
 MESSAGE = 16
 NEGATIVE = -(2.0**100)
@@ -274,7 +275,7 @@
         verify_ref[j] = rounded[j * BATCH : (j + 1) * BATCH]
     for k, half in enumerate(halves):
         at = slice(k * LANES, (k + 1) * LANES)
-        half[...] = summed[TOKENS:, at]
+        half[pl.ds(0, DRAFT * BATCH), :] = summed[TOKENS:, at]
         for b in range(BATCH):
             draft_ref[b, :, at] = half[pl.ds(b, DRAFT, stride=BATCH), :].astype(BF16)
 
@@ -316,7 +317,7 @@
     parts, cosine, sine, live, kept, fresh = pl.pallas_call(
         project,
         out_shape=(
-            array((SEQ, MESSAGE, LANES), BF16),
+            array((SEQ, MESSAGE, LANES), F32),
             array((MESSAGE, LANES), F32),
             array((MESSAGE, LANES), F32),
             array((BATCH, context), F32),
@@ -368,8 +369,8 @@
         scratch_shapes=[
             pltpu.VMEM((BATCH, VERIFY * ROWS, context), F32),
             pltpu.VMEM((BATCH, TILES * ROWS, context), BF16),
-            pltpu.VMEM((BATCH * TILES * ROWS, LANES), F32),
-            pltpu.VMEM((SEQ * SUB, LANES), F32),
+            pltpu.VMEM((BATCH * TILES * ROWS + SPARE, LANES), F32),
+            pltpu.VMEM((SEQ * SUB + SPARE, LANES), F32),
         ],
         name="attend",
         compiler_params=pltpu.CompilerParams(vmem_limit_bytes=16 << 20),
@@ -387,7 +388,7 @@
         out_shape=pltpu.VMEM((SEQ, SUB, STRIPS * LANES), BF16),
         in_specs=[VMEM],
         out_specs=VMEM,
-        scratch_shapes=[pltpu.VMEM((SEQ * SLOTS, LANES), F32)],
+        scratch_shapes=[pltpu.VMEM((SEQ * SLOTS + SPARE, LANES), F32)],
         name="merge",
         compiler_params=pltpu.CompilerParams(vmem_limit_bytes=8 << 20),
     )(resident(partial))
@@ -397,7 +398,7 @@
         out_shape=pltpu.VMEM((BATCH * TILES, columns), BF16),
         in_specs=[VMEM, VMEM],
         out_specs=VMEM,
-        scratch_shapes=[pltpu.VMEM((BATCH * TILES * ROWS, LANES), F32)],
+        scratch_shapes=[pltpu.VMEM((BATCH * TILES * ROWS + SPARE, LANES), F32)],
         name="project_out",
         compiler_params=pltpu.CompilerParams(vmem_limit_bytes=8 << 20),
     )(resident(merged), resident(w_out))
@@ -420,7 +421,7 @@
         ),
         in_specs=[VMEM],
         out_specs=(VMEM, VMEM),
-        scratch_shapes=[pltpu.VMEM((DRAFT * BATCH, LANES), F32)] * (columns // LANES),
+        scratch_shapes=[pltpu.VMEM((DRAFT * BATCH + SPARE, LANES), F32)] * (columns // LANES),
         name="add_groups",
         compiler_params=pltpu.CompilerParams(vmem_limit_bytes=8 << 20),
     )(resident(pairs))

time: 80.6 us -> 83.3 us (1.033)
  blocking collectives: 68.6 us -> 71.9 us
    all_to_all x4, blocking collectives: 59.9 us -> 63.1 us  [exchange(): return lax.all_to_all(messages, axis, 0, 0, tiled=True)]
where the time goes in v6:
time: 83.3 us; the launch traced here: 83 us
  blocking collectives  71.9 us (86%)
  starting transfers between devices  5.18 us (6%)
  Pallas kernels  4.42 us (5%)
  waiting for transfers between devices  0.87 us (1%)
    all_to_all x4, blocking collectives, exchange(): return lax.all_to_all(messages, axis, 0, 0, tiled=True)  63.1 us
    all_to_all x1, blocking collectives, per_device(): lax.all_to_all(pairs, 'head', 0, 0, tiled=True, axis_index_groups=across)  8.72 us
    ppermute x1, starting transfers between devices, per_device(): other = lax.ppermute(groups, 'head', [(h, h ^ 1) for h in range(HEADS)])  5.18 us
  transfers between devices with their start and end apart: 1, of which 1 were waited for; matrix products, arithmetic and copies ran while one was open for 0% of the time, Pallas kernels for 0%

profile of v6, /device:TPU:1, one launch (start us, length us, event | category | flops | bytes accessed | tf_op | source)
XLA Modules:
  0.0 83.0 jit_solution(6292263792217860564)
XLA Ops:
  0.6 1.4 %project.1 = (f32[32,16,128]{2,1,0:T(8,128)S(1)}, f32[16,128]{1,0:T(8,128)S(1)}, f32[16,128]{1,0:T(8,128)S(1)}, f32[8,1024]{1,0:T(8,128)S(1)}, f32[8,1024]{1,0:T(8,128)S(1)}, /*index=5*/f32[8,128]{1,0:T(8,128)S(1)}) custom-call(bf16[40,256]{1,0:T(8,128)(2,1)} %bitcast.6, bf16[256,1024]{1,0:T(8,128)(2,1)} %query_hbm.1, bf16[256,128]{1,0:T(8,128)(2,1)} %key_hbm.1, ...), custom_call_target="tpu_custom_call" | custom-call | tf_op jit(solution)/shard_map/project/pallas_call | solution.py:317
  2.0 0.0 copy-start.1
  2.0 23.3 %all_to_all.25.parts_ref = f32[32,16,128]{2,1,0:T(8,128)S(1)} all-to-all(f32[32,16,128]{2,1,0:T(8,128)S(1)} %get-tuple-element.13), channel_id=1, replica_groups=mesh['seq'=32,'head'=8] {'seq'}, dimensions={0} | all-to-all | bytes 524288 | tf_op jit(solution)/shard_map/all_to_all | solution.py:296
  25.3 0.0 copy-start
  25.3 0.1 rotate.1
  25.4 14.0 %all_to_all.26 = bf16[32,16,128]{2,1,0:T(8,128)(2,1)S(1)} all-to-all(bf16[32,16,128]{2,1,0:T(8,128)(2,1)S(1)} %rotate.1), channel_id=1, replica_groups=mesh['seq'=32,'head'=8] {'seq'}, dimensions={0} | all-to-all | bytes 262144 | tf_op jit(solution)/shard_map/all_to_all | solution.py:296
  39.4 0.0 copy-done.1
  39.4 0.0 copy-done
  39.4 0.0 copy-start.2
  39.4 1.6 %attend.1 = bf16[32,4,640]{2,1,0:T(4,128)(2,1)S(1)} custom-call(f32[8,1024]{1,0:T(8,128)S(1)} %get-tuple-element.10.live_ref, f32[8,1024]{1,0:T(8,128)S(1)} %get-tuple-element.11.kept_ref, f32[8,128]{1,0:T(8,128)S(1)} %get-tuple-element.12.fresh_ref, bf16[512,128]{1,0:T(8,128)(2,1)S(1)} %bitcast.5, bf16[8,1024,128]{2,1,0:T(8,128)(2,1)S(1)} %copy-done, ...), custom_call_target="tpu_custom_call" | custom-call | tf_op jit(solution)/shard_map/attend/pallas_call | solution.py:364
  41.0 12.9 %all_to_all.27.parts_ref = bf16[32,4,640]{2,1,0:T(4,128)(2,1)S(1)} all-to-all(bf16[32,4,640]{2,1,0:T(4,128)(2,1)S(1)} %attend.1), channel_id=1, replica_groups=mesh['seq'=32,'head'=8] {'seq'}, dimensions={0} | all-to-all | bytes 327680 | tf_op jit(solution)/shard_map/all_to_all | solution.py:296
  53.9 0.4 merge.1
  54.3 13.0 %all_to_all.28.all_ref = bf16[32,4,640]{2,1,0:T(4,128)(2,1)S(1)} all-to-all(bf16[32,4,640]{2,1,0:T(4,128)(2,1)S(1)} %merge.1), channel_id=1, replica_groups=mesh['seq'=32,'head'=8] {'seq'}, dimensions={0} | all-to-all | bytes 327680 | tf_op jit(solution)/shard_map/all_to_all | solution.py:296
  67.3 0.0 copy-done.2
  67.3 0.3 project_out.1.mine_ref
  67.6 5.2 %collective-permute-start = (bf16[72,256]{1,0:T(8,128)(2,1)S(1)}, bf16[72,256]{1,0:T(8,128)(2,1)S(1)}, u32[]{:S(2)}, u32[]{:S(2)}) collective-permute-start(bf16[72,256]{1,0:T(8,128)(2,1)S(1)} %project_out.1.mine_ref), channel_id=1, source_target_pairs={{0,1},{1,0},{2,3},{3,2},{4,5},{5,4},{6,7},{7,6},{8,9},{9,8},{10,11... | collective-permute-start | bytes 110600 | tf_op jit(solution)/shard_map/ppermute | solution.py:405
  72.8 0.9 %collective-permute-done.other_ref = bf16[72,256]{1,0:T(8,128)(2,1)S(1)} collective-permute-done((bf16[72,256]{1,0:T(8,128)(2,1)S(1)}, bf16[72,256]{1,0:T(8,128)(2,1)S(1)}, u32[]{:S(2)}, u32[]{:S(2)}) %collective-permute-start) | collective-permute-done | bytes 36896 | tf_op jit(solution)/shard_map/ppermute | solution.py:405
  73.7 8.7 %all_to_all.29.parts_ref = bf16[4,72,256]{2,1,0:T(8,128)(2,1)S(1)} all-to-all(bf16[4,72,256]{2,1,0:T(8,128)(2,1)S(1)} %add_pair.1), channel_id=1, replica_groups={{0,2,4,6},{1,3,5,7},{8,10,12,14},{9,11,13,15},{16,18,20,22},{17,19,21,2..., dimensions={0} | all-to-all | bytes 294912 | tf_op jit(solution)/shard_map/all_to_all | solution.py:415
  82.4 0.6 add_groups.1
  (1 shorter events, 0.0 us)
Async XLA Ops:
  2.0 37.4 %copy-start.1 = (bf16[8,1024,128]{2,1,0:T(8,128)(2,1)S(1)}, bf16[8,1024,128]{2,1,0:T(8,128)(2,1)}, u32[]{:S(2)}) copy-start(bf16[8,1024,128]{2,1,0:T(8,128)(2,1)} %values.1) | copy-start | bytes 6291460
  25.3 14.1 %copy-start = (bf16[8,1024,128]{2,1,0:T(8,128)(2,1)S(1)}, bf16[8,1024,128]{2,1,0:T(8,128)(2,1)}, u32[]{:S(2)}) copy-start(bf16[8,1024,128]{2,1,0:T(8,128)(2,1)} %keys.1) | copy-start | bytes 6291460
  39.4 27.9 %copy-start.2 = (bf16[1024,256]{1,0:T(8,128)(2,1)S(1)}, bf16[1024,256]{1,0:T(8,128)(2,1)}, u32[]{:S(2)}) copy-start(bf16[1024,256]{1,0:T(8,128)(2,1)} %weight_ref.1) | copy-start | bytes 1572868
  67.6 6.0 %collective-permute-start = (bf16[72,256]{1,0:T(8,128)(2,1)S(1)}, bf16[72,256]{1,0:T(8,128)(2,1)S(1)}, u32[]{:S(2)}, u32[]{:S(2)}) collective-permute-start(bf16[72,256]{1,0:T(8,128)(2,1)S(1)} %project_out.1.mine_ref), channel_id=1, source_target_pairs={{0,1},{1,0},{2,3},{3,2},{4,5},{5,4},{6,7},{7,6},{8,9},{9,8},{10,11... | collective-permute-start | bytes 110600 | tf_op jit(solution)/shard_map/ppermute | solution.py:405

commit v7 on v6

--- a/solution.py
+++ b/solution.py
@@ -24,6 +24,7 @@
 STRIPS = 5
 SPARE = 72
 SLOTS = 24
+QUERIES = QUERY_ROWS // SEQ
 MESSAGE = 16
 NEGATIVE = -(2.0**100)
 SCALE = LANES**-0.5
@@ -35,7 +36,7 @@
 def project(
     hidden_hbm, query_hbm, key_hbm, value_hbm, lengths_hbm, keep_hbm, inverse_hbm,
     out_ref, cosine_ref, sine_ref, live_ref, kept_ref, fresh_ref,
-    hidden_ref, query_ref, key_ref, value_ref, lengths_ref, keep_ref, inverse_ref, flat, sems,
+    hidden_ref, query_ref, key_ref, value_ref, lengths_ref, keep_ref, inverse_ref, flat, packed, sems,
 ):
     pairs = (
         (lengths_hbm, lengths_ref),
@@ -60,18 +61,22 @@
     lengths = jnp.zeros((ROWS, LANES), jnp.int32)
     for b in range(BATCH):
         lengths = jnp.where(row == b, lengths_ref[b], lengths)
-    for half in range(MESSAGE // ROWS):
-        tile = here * (MESSAGE // ROWS) + half
-        is_query = tile < TOKENS
-        token = jnp.where(is_query, tile, 0)
-        query_position = lengths_ref[lax.rem(token, BATCH)] + token // BATCH
-        position = jnp.where(is_query, query_position, lengths + (tile - TOKENS))
-        angle = position.astype(F32) * inverse_ref[...]
-        plain = tile >= TOKENS + VERIFY
-        at = slice(half * ROWS, (half + 1) * ROWS)
-        sine = jnp.sin(angle)
-        cosine_ref[at, :] = jnp.where(plain, 1.0, jnp.cos(angle))
-        sine_ref[at, :] = jnp.where(plain, 0.0, jnp.where(lane < LANES // 2, -sine, sine))
+    mine, turn = here // OWNERS, lax.rem(here, OWNERS)
+    slot = lax.broadcasted_iota(jnp.int32, (MESSAGE, LANES), 0)
+    token = jnp.where(
+        slot < QUERIES,
+        jnp.right_shift(QUERIES * here + slot, 3),
+        jnp.where(slot < QUERIES + 2, turn * BATCH + mine, DRAFT * BATCH + mine),
+    )
+    position = jnp.right_shift(token, 3)
+    for b in range(BATCH):
+        position += jnp.where(jnp.bitwise_and(token, 7) == b, lengths_ref[b], 0)
+    angle = position.astype(F32) * inverse_ref[...]
+    plain = (slot == QUERIES + 1) | (slot == QUERIES + 3)
+    half = lax.broadcasted_iota(jnp.int32, (MESSAGE, LANES), 1) < LANES // 2
+    sine = jnp.sin(angle)
+    cosine_ref[...] = jnp.where(plain, 1.0, jnp.cos(angle))
+    sine_ref[...] = jnp.where(plain, 0.0, jnp.where(half, -sine, sine))
     blocks = live_ref.shape[1] // LANES
     for c in range(blocks):
         at = slice(c * LANES, (c + 1) * LANES)
@@ -81,7 +86,9 @@
         for b in range(BATCH):
             keep = jnp.where(row == b, keep_ref[b, c], keep)
         kept_ref[:, at] = jnp.where(keep > 0, 0.0, NEGATIVE)
-    fresh_ref[...] = jnp.full((ROWS, LANES), jnp.where(here == 0, 0.0, NEGATIVE))
+    fresh_ref[pl.ds(0, ROWS), :] = jnp.where(row == mine, 0.0, NEGATIVE)
+    seen = ((lane == 0) & (turn <= row)) | ((lane == 1) & (row == DRAFT) & (turn == 0))
+    fresh_ref[pl.ds(ROWS, ROWS), :] = jnp.where(seen, 0.0, NEGATIVE)
     for load in loads[3:]:
         load.wait()
     rows = hidden_ref[...]
@@ -92,19 +99,30 @@
     flat[pl.ds(QUERY_ROWS + TOKENS, TOKENS), :] = jnp.dot(
         rows, value_ref[...], preferred_element_type=F32
     )
-    used = QUERY_ROWS + 2 * TOKENS
-    flat[pl.ds(used, SEQ * MESSAGE - used), :] = jnp.zeros((SEQ * MESSAGE - used, LANES), F32)
-    out_ref[...] = flat[...].reshape(SEQ, MESSAGE, LANES).astype(out_ref.dtype)
-
-
-def rotate(parts_ref, cosine_ref, sine_ref, out_ref):
+    for d in range(SEQ):
+        packed[pl.ds(d * MESSAGE + ROWS, ROWS), :] = jnp.zeros((ROWS, LANES), F32)
+        packed[pl.ds(d * MESSAGE, QUERIES), :] = flat[pl.ds(d * QUERIES, QUERIES), :]
+    for j in range(VERIFY):
+        first = (j % OWNERS) * MESSAGE + QUERIES + 2 * (j // OWNERS)
+        for k in range(2):
+            packed[pl.ds(first + k, BATCH, stride=OWNERS * MESSAGE), :] = flat[
+                pl.ds(QUERY_ROWS + k * TOKENS + j * BATCH, BATCH), :
+            ]
+    parts = packed[pl.ds(0, SEQ * MESSAGE), :]
+    out_ref[...] = parts.reshape(SEQ, MESSAGE, LANES).astype(out_ref.dtype)
+
+
+def rotate(parts_ref, cosine_ref, sine_ref, out_ref, own_ref):
     total = parts_ref[0].astype(F32)
     for s in range(1, SEQ):
         total += parts_ref[s].astype(F32)
     swapped = pltpu.roll(total, LANES // 2, 1)
-    rotated = (total * cosine_ref[...] + swapped * sine_ref[...]).astype(BF16)
-    for s in range(SEQ):
-        out_ref[s] = rotated
+    rotated = total * cosine_ref[...] + swapped * sine_ref[...]
+    own_ref[...] = rotated[ROWS:]
+    for k in range(QUERIES // 2):
+        strip = rotated[2 * k : 2 * k + 2].astype(BF16)
+        for s in range(SEQ):
+            out_ref[s, :, k * LANES : (k + 1) * LANES] = strip
 
 
 def split(value):
@@ -113,15 +131,32 @@
 
 
 def attend(
-    live_ref, kept_ref, fresh_ref, all_ref, keys, values,
-    out_ref, scores, weights, results, tails,
+    live_ref, kept_ref, fresh_ref, own_ref, spread_ref, keys, values,
+    out_ref, scores, weights, results, tails, all_ref,
 ):
     blocks = keys.shape[1] // LANES
     lane = lax.broadcasted_iota(jnp.int32, (ROWS, LANES), 1)
-    lane_row = lax.rem(lane, BATCH)
-    padding = jnp.zeros((LANES - TOKENS, LANES), BF16)
-    new_keys = jnp.concatenate([all_ref[pl.ds(QUERY_ROWS, TOKENS), :], padding], axis=0)
-    new_values = jnp.concatenate([all_ref[pl.ds(QUERY_ROWS + TOKENS, TOKENS), :], padding], axis=0)
+    row = lax.broadcasted_iota(jnp.int32, (ROWS, LANES), 0)
+    own = own_ref[...]
+    first = QUERIES - ROWS
+    new_keys, new_values = (
+        jnp.concatenate(
+            [
+                jnp.where(
+                    row == 0,
+                    own[first + k : first + k + 1],
+                    jnp.where(row == 1, own[first + k + 2 : first + k + 3], 0.0),
+                ),
+                jnp.zeros((LANES - ROWS, LANES), F32),
+            ],
+            axis=0,
+        ).astype(BF16)
+        for k in range(2)
+    )
+    for d in range(SEQ):
+        for k in range(QUERIES // 2):
+            strip = spread_ref[d, :, k * LANES : (k + 1) * LANES]
+            all_ref[pl.ds(d * QUERIES + 2 * k, 2), :] = strip.astype(F32)
     transposed = (((1,), (1,)), ((), ()))
     exponent = SCALE * LOG2E
 
@@ -130,12 +165,12 @@
 
     new_scores = (
         lax.dot_general(
-            all_ref[pl.ds(0, QUERY_ROWS), :], new_keys, transposed, preferred_element_type=F32
+            all_ref[...].astype(BF16), new_keys, transposed, preferred_element_type=F32
         )
         * exponent
     )
     for b in range(BATCH):
-        query = jnp.concatenate([all_ref[tile(j, b), :] for j in range(VERIFY)], axis=0)
+        query = jnp.concatenate([all_ref[tile(j, b), :] for j in range(VERIFY)], axis=0).astype(BF16)
         scores[b] = (
             lax.dot_general(query, keys[b], transposed, preferred_element_type=F32) * exponent
             + live_ref[b : b + 1, :]
@@ -146,8 +181,8 @@
         rows = []
         for j in range(VERIFY):
             at = (j * BATCH + b) * ROWS
-            seen = (lane_row == b) & (lane < (j + 1) * BATCH)
-            rows.append(jnp.where(seen, new_scores[at : at + ROWS] + fresh_ref[...], NEGATIVE))
+            bias = fresh_ref[b : b + 1, :] + fresh_ref[ROWS + j : ROWS + j + 1, :]
+            rows.append(new_scores[at : at + ROWS] + bias)
         rows = jnp.concatenate(rows, axis=0)
         target, draft = rows, rows[: DRAFT * ROWS]
         fresh.append(jnp.concatenate([target, draft], axis=0))
@@ -317,12 +352,12 @@
     parts, cosine, sine, live, kept, fresh = pl.pallas_call(
         project,
         out_shape=(
-            array((SEQ, MESSAGE, LANES), F32),
+            array((SEQ, MESSAGE, LANES), BF16),
             array((MESSAGE, LANES), F32),
             array((MESSAGE, LANES), F32),
             array((BATCH, context), F32),
             array((BATCH, context), F32),
-            array((ROWS, LANES), F32),
+            array((2 * ROWS, LANES), F32),
         ),
         in_specs=[HBM] * 7,
         out_specs=(VMEM,) * 6,
@@ -334,7 +369,8 @@
             pltpu.SMEM(context_lengths.shape, jnp.int32),
             pltpu.SMEM(keep_blocks.shape, jnp.int32),
             pltpu.VMEM((1, LANES), F32),
-            pltpu.VMEM((SEQ * MESSAGE, LANES), F32),
+            pltpu.VMEM((QUERY_ROWS + 2 * TOKENS, LANES), F32),
+            pltpu.VMEM((SEQ * MESSAGE + SPARE, LANES), F32),
             pltpu.SemaphoreType.DMA((7,)),
         ],
         name="project",
@@ -349,11 +385,14 @@
         )
     )
     parts = exchange(parts, "seq")
-    rotated = pl.pallas_call(
+    rotated, own = pl.pallas_call(
         rotate,
-        out_shape=pltpu.VMEM((SEQ, MESSAGE, LANES), BF16),
+        out_shape=(
+            pltpu.VMEM((SEQ, 2, QUERIES // 2 * LANES), BF16),
+            pltpu.VMEM((ROWS, LANES), F32),
+        ),
         in_specs=[VMEM] * 3,
-        out_specs=VMEM,
+        out_specs=(VMEM, VMEM),
         name="rotate",
         cost_estimate=pl.CostEstimate(
             flops=1000000000, transcendentals=0, bytes_accessed=64000000
@@ -364,13 +403,14 @@
     partial = pl.pallas_call(
         attend,
         out_shape=pltpu.VMEM((SEQ, SUB, STRIPS * LANES), BF16),
-        in_specs=[VMEM] * 6,
+        in_specs=[VMEM] * 7,
         out_specs=VMEM,
         scratch_shapes=[
             pltpu.VMEM((BATCH, VERIFY * ROWS, context), F32),
             pltpu.VMEM((BATCH, TILES * ROWS, context), BF16),
             pltpu.VMEM((BATCH * TILES * ROWS + SPARE, LANES), F32),
             pltpu.VMEM((SEQ * SUB + SPARE, LANES), F32),
+            pltpu.VMEM((QUERY_ROWS, LANES), F32),
         ],
         name="attend",
         compiler_params=pltpu.CompilerParams(vmem_limit_bytes=16 << 20),
@@ -378,7 +418,8 @@
         resident(live),
         resident(kept),
         resident(fresh),
-        resident(rotated.reshape(SEQ * MESSAGE, LANES)),
+        resident(own),
+        resident(rotated),
         resident(key_cache),
         resident(value_cache),
     )

time: 83.3 us -> 80.2 us (0.963)
  blocking collectives: 71.9 us -> 67.9 us
    all_to_all x4, blocking collectives: 63.1 us -> 59.2 us  [exchange(): return lax.all_to_all(messages, axis, 0, 0, tiled=True)]
where the time goes in v7:
time: 80.2 us; the launch traced here: 79.9 us
  blocking collectives  67.9 us (85%)
  starting transfers between devices  5.71 us (7%)
  Pallas kernels  4.69 us (6%)
  waiting for transfers between devices  0.87 us (1%)
    all_to_all x4, blocking collectives, exchange(): return lax.all_to_all(messages, axis, 0, 0, tiled=True)  59.2 us
    all_to_all x1, blocking collectives, per_device(): lax.all_to_all(pairs, 'head', 0, 0, tiled=True, axis_index_groups=across)  8.73 us
    ppermute x1, starting transfers between devices, per_device(): other = lax.ppermute(groups, 'head', [(h, h ^ 1) for h in range(HEADS)])  5.71 us
    pallas_call x1, Pallas kernels, per_device(): pl.pallas_call(attend, out_shape=pltpu.VMEM((SEQ, SUB, STRIPS * LANES), B...  1.63 us
  transfers between devices with their start and end apart: 1, of which 1 were waited for; matrix products, arithmetic and copies ran while one was open for 0% of the time, Pallas kernels for 0%

profile of v7, /device:TPU:1, one launch (start us, length us, event | category | flops | bytes accessed | tf_op | source)
XLA Modules:
  0.0 79.9 jit_solution(15025743608482441650)
XLA Ops:
  0.6 0.0 copy-start.1
  0.6 1.6 %project.1 = (bf16[32,16,128]{2,1,0:T(8,128)(2,1)S(1)}, f32[16,128]{1,0:T(8,128)S(1)}, f32[16,128]{1,0:T(8,128)S(1)}, f32[8,1024]{1,0:T(8,128)S(1)}, f32[8,1024]{1,0:T(8,128)S(1)}, /*index=5*/f32[16,128]{1,0:T(8,128)S(1)}) custom-call(bf16[40,256]{1,0:T(8,128)(2,1)} %bitcast.4, bf16[256,1024]{1,0:T(8,128)(2,1)} %query_hbm.1, bf16[256,128]{1,0:T(8,128)(2,1)} %key_hbm.1, ...), custom_call_target="tpu_custom_call" | custom-call | tf_op jit(solution)/shard_map/project/pallas_call | solution.py:352
  2.2 0.0 copy-start
  2.2 21.3 %all_to_all.25.parts_ref = bf16[32,16,128]{2,1,0:T(8,128)(2,1)S(1)} all-to-all(bf16[32,16,128]{2,1,0:T(8,128)(2,1)S(1)} %get-tuple-element.15), channel_id=1, replica_groups=mesh['seq'=32,'head'=8] {'seq'}, dimensions={0} | all-to-all | bytes 262144 | tf_op jit(solution)/shard_map/all_to_all | solution.py:331
  23.5 0.1 rotate.1
  23.7 12.3 %all_to_all.26.spread_ref = bf16[32,2,640]{2,1,0:T(2,128)(2,1)S(1)} all-to-all(bf16[32,2,640]{2,1,0:T(2,128)(2,1)S(1)} %get-tuple-element.19), channel_id=1, replica_groups=mesh['seq'=32,'head'=8] {'seq'}, dimensions={0} | all-to-all | bytes 163840 | tf_op jit(solution)/shard_map/all_to_all | solution.py:331
  35.9 0.0 copy-done.1
  35.9 0.0 copy-done
  35.9 0.0 copy-start.2
  35.9 1.6 %attend.1 = bf16[32,4,640]{2,1,0:T(4,128)(2,1)S(1)} custom-call(f32[8,1024]{1,0:T(8,128)S(1)} %get-tuple-element.12.live_ref, f32[8,1024]{1,0:T(8,128)S(1)} %get-tuple-element.13.kept_ref, f32[16,128]{1,0:T(8,128)S(1)} %get-tuple-element.14.fresh_ref, f32[8,128]{1,0:T(8,128)S(1)} %get-tuple-element.18.own_ref, ...), custom_call_target="tpu_custom_call" | custom-call | tf_op jit(solution)/shard_map/attend/pallas_call | solution.py:403
  37.6 12.9 %all_to_all.27.parts_ref = bf16[32,4,640]{2,1,0:T(4,128)(2,1)S(1)} all-to-all(bf16[32,4,640]{2,1,0:T(4,128)(2,1)S(1)} %attend.1), channel_id=1, replica_groups=mesh['seq'=32,'head'=8] {'seq'}, dimensions={0} | all-to-all | bytes 327680 | tf_op jit(solution)/shard_map/all_to_all | solution.py:331
  50.4 0.4 merge.1
  50.9 12.8 %all_to_all.28.all_ref = bf16[32,4,640]{2,1,0:T(4,128)(2,1)S(1)} all-to-all(bf16[32,4,640]{2,1,0:T(4,128)(2,1)S(1)} %merge.1), channel_id=1, replica_groups=mesh['seq'=32,'head'=8] {'seq'}, dimensions={0} | all-to-all | bytes 327680 | tf_op jit(solution)/shard_map/all_to_all | solution.py:331
  63.7 0.0 copy-done.2
  63.7 0.3 project_out.1.mine_ref
  64.0 5.7 %collective-permute-start = (bf16[72,256]{1,0:T(8,128)(2,1)S(1)}, bf16[72,256]{1,0:T(8,128)(2,1)S(1)}, u32[]{:S(2)}, u32[]{:S(2)}) collective-permute-start(bf16[72,256]{1,0:T(8,128)(2,1)S(1)} %project_out.1.mine_ref), channel_id=1, source_target_pairs={{0,1},{1,0},{2,3},{3,2},{4,5},{5,4},{6,7},{7,6},{8,9},{9,8},{10,11... | collective-permute-start | bytes 110600 | tf_op jit(solution)/shard_map/ppermute | solution.py:446
  69.7 0.9 %collective-permute-done.other_ref = bf16[72,256]{1,0:T(8,128)(2,1)S(1)} collective-permute-done((bf16[72,256]{1,0:T(8,128)(2,1)S(1)}, bf16[72,256]{1,0:T(8,128)(2,1)S(1)}, u32[]{:S(2)}, u32[]{:S(2)}) %collective-permute-start) | collective-permute-done | bytes 36896 | tf_op jit(solution)/shard_map/ppermute | solution.py:446
  70.5 8.7 %all_to_all.29.parts_ref = bf16[4,72,256]{2,1,0:T(8,128)(2,1)S(1)} all-to-all(bf16[4,72,256]{2,1,0:T(8,128)(2,1)S(1)} %add_pair.1), channel_id=1, replica_groups={{0,2,4,6},{1,3,5,7},{8,10,12,14},{9,11,13,15},{16,18,20,22},{17,19,21,2..., dimensions={0} | all-to-all | bytes 294912 | tf_op jit(solution)/shard_map/all_to_all | solution.py:456
  79.3 0.6 add_groups.1
  (1 shorter events, 0.0 us)
Async XLA Ops:
  0.6 35.3 %copy-start.1 = (bf16[8,1024,128]{2,1,0:T(8,128)(2,1)S(1)}, bf16[8,1024,128]{2,1,0:T(8,128)(2,1)}, u32[]{:S(2)}) copy-start(bf16[8,1024,128]{2,1,0:T(8,128)(2,1)} %values.1) | copy-start | bytes 6291460
  2.2 33.7 %copy-start = (bf16[8,1024,128]{2,1,0:T(8,128)(2,1)S(1)}, bf16[8,1024,128]{2,1,0:T(8,128)(2,1)}, u32[]{:S(2)}) copy-start(bf16[8,1024,128]{2,1,0:T(8,128)(2,1)} %keys.1) | copy-start | bytes 6291460
  35.9 27.8 %copy-start.2 = (bf16[1024,256]{1,0:T(8,128)(2,1)S(1)}, bf16[1024,256]{1,0:T(8,128)(2,1)}, u32[]{:S(2)}) copy-start(bf16[1024,256]{1,0:T(8,128)(2,1)} %weight_ref.1) | copy-start | bytes 1572868
  64.0 6.6 %collective-permute-start = (bf16[72,256]{1,0:T(8,128)(2,1)S(1)}, bf16[72,256]{1,0:T(8,128)(2,1)S(1)}, u32[]{:S(2)}, u32[]{:S(2)}) collective-permute-start(bf16[72,256]{1,0:T(8,128)(2,1)S(1)} %project_out.1.mine_ref), channel_id=1, source_target_pairs={{0,1},{1,0},{2,3},{3,2},{4,5},{5,4},{6,7},{7,6},{8,9},{9,8},{10,11... | collective-permute-start | bytes 110600 | tf_op jit(solution)/shard_map/ppermute | solution.py:446
